TPU v7x, 128 devices: a whole 4x4x4 slice. The times are simulated.
128 devices in a mesh: cell: 64 (over y, z, x), qgrp: 2 (over core).
Axes of the slice: x: 4, y: 4, z: 4, core: 2. Of those that a mesh axis runs over, the one named last changes fastest.
Arguments:
- supernode_embeddings: bfloat16 [32768, 768], P('cell'), may hold values from -6 to 6
- filled_supernode_tally: int32 [64], P('cell'), may hold values from 1 to 512, 24576 in all
- hidden_probe_states: bfloat16 [1024, 768], replicated, may hold values from -6 to 6
- softness_per_channel: float32 [2, 12], replicated, may hold values from 1 to 12, as said below
- gather_probe_projector: bfloat16 [768, 768], P(None, 'qgrp'), may hold values from -0.4375 to 0.4375
- gather_lookup_projector: bfloat16 [768, 768], P(None, 'qgrp'), may hold values from -0.4375 to 0.4375
- gather_content_projector: bfloat16 [768, 768], P(None, 'qgrp'), may hold values from -0.21875 to 0.21875
- gather_final_projector: bfloat16 [768, 768], P('qgrp'), may hold values from -0.21875 to 0.21875
- unpack_probe_projector: bfloat16 [768, 768], P(None, 'qgrp'), may hold values from -0.21875 to 0.21875
- unpack_lookup_projector: bfloat16 [768, 768], P(None, 'qgrp'), may hold values from -0.21875 to 0.21875
- unpack_content_projector: bfloat16 [768, 768], P(None, 'qgrp'), may hold values from -0.21875 to 0.21875
- unpack_final_projector: bfloat16 [768, 768], P('qgrp'), may hold values from -0.21875 to 0.21875
- hidden_state_gain: float32 [768], replicated, may hold values from 0.1 to 1.9
Outputs:
- latent_out: float32 [1024, 768], replicated
- tokens_out: float32 [32768, 768], P(('cell', 'qgrp'))
Inputs may be any that keep to these rules, and one draw needn't show every extreme that they name: Slots 0 to filled_supernode_tally[c] - 1 of cell block c hold its valid supernodes; its other slots are padding. `softness_per_channel`: A positive temperature for each head.
All inputs are finite; a program needn't handle non-finite values.
Results may differ from a plain program's by a relative error of at most 0.009.
The roundings to bfloat16 on the way count: a program that leaves them out, or rounds other values in their place, can miss the bound.
Values may be sent and summed in bfloat16 or wider, within the bound.
A program may use at most 448 MiB of HBM per device.

v0:
```python
import math

import jax
import jax.numpy as jnp
from jax import lax
from jax.sharding import PartitionSpec as P

D = 768
HEADS = 12


MASKED_SCORE = -1e30
NORM_EPSILON = 1e-06


def combined_all(value, axis, join):
    pieces = jax.tree.map(lambda part: lax.all_gather(part, axis), value)
    head = jax.tree.map(lambda part: part[0], pieces)
    tail = jax.tree.map(lambda part: part[1:], pieces)
    total, _ = lax.scan(lambda total, piece: (join(total, piece), None), head, tail)
    return total


def rms_norm(values, gain):
    mean_square = jnp.mean(values * values, axis=-1, keepdims=True)
    return values * lax.rsqrt(mean_square + NORM_EPSILON) * gain


def masked_scores(queries, key_rows, score_scale, is_valid):
    scores = (
        jnp.einsum("lhd,khd->lhk", queries, key_rows, preferred_element_type=jnp.float32)
        * score_scale[None, :, None]
    )
    return jnp.where(is_valid[None, None, :], scores, jnp.float32(MASKED_SCORE))


def combine_partials(left_part, right_part):
    left_max, left_sum, left_acc = left_part
    right_max, right_sum, right_acc = right_part
    per_channel_dimension = left_acc.shape[1] // left_max.shape[1]
    both_max = jnp.maximum(left_max, right_max)
    left_factor = jnp.exp(left_max - both_max)
    right_factor = jnp.exp(right_max - both_max)
    both_sum = left_sum * left_factor + right_sum * right_factor
    both_acc = left_acc * jnp.repeat(
        left_factor, per_channel_dimension, axis=1
    ) + right_acc * jnp.repeat(right_factor, per_channel_dimension, axis=1)
    return (both_max, both_sum, both_acc)


def decode_rows(
    row_data, q_weight, k_weight, v_weight, score_scale, latent_half, per_channel_dimension
):
    row_total = row_data.shape[0]
    latent_rows = latent_half.shape[0]
    heads_here = q_weight.shape[1] // per_channel_dimension
    dec_queries = (
        jnp.dot(row_data, q_weight, preferred_element_type=jnp.float32)
        .astype(jnp.bfloat16)
        .reshape(row_total, heads_here, per_channel_dimension)
    )
    dec_keys = (
        jnp.dot(latent_half, k_weight, preferred_element_type=jnp.float32)
        .astype(jnp.bfloat16)
        .reshape(latent_rows, heads_here, per_channel_dimension)
    )
    dec_values = (
        jnp.dot(latent_half, v_weight, preferred_element_type=jnp.float32)
        .astype(jnp.bfloat16)
        .reshape(latent_rows, heads_here, per_channel_dimension)
    )
    row_block = math.gcd(row_total, 512)

    def visit(block_index, buffer):
        scores = (
            jnp.einsum("khd,lhd->khl", dec_queries, dec_keys, preferred_element_type=jnp.float32)
            * score_scale[None, :, None]
        )
        weights = jnp.exp(scores - jnp.max(scores, axis=-1, keepdims=True))
        denominator = jnp.sum(weights, axis=-1)
        mixed_heads = (
            jnp.einsum(
                "khl,lhd->khd",
                weights.astype(jnp.bfloat16),
                dec_values,
                preferred_element_type=jnp.float32,
            )
            / denominator[:, :, None]
        )
        mixed_heads = mixed_heads.astype(jnp.bfloat16).reshape(
            row_block, heads_here * per_channel_dimension
        )
        return mixed_heads

    buffer = jnp.zeros((row_total, heads_here * per_channel_dimension), jnp.bfloat16)
    block_count = row_total // row_block
    return lax.fori_loop(0, block_count, visit, buffer)


def body(
    supernode_embeddings,
    filled_supernode_tally,
    hidden_probe_states,
    softness_per_channel,
    gather_probe_projector,
    gather_lookup_projector,
    gather_content_projector,
    gather_final_projector,
    unpack_probe_projector,
    unpack_lookup_projector,
    unpack_content_projector,
    unpack_final_projector,
    hidden_state_gain,
):
    per_channel_dimension = D // HEADS
    local_channel_total = gather_probe_projector.shape[1] // per_channel_dimension
    slot_count = supernode_embeddings.shape[0]
    latent_rows = hidden_probe_states.shape[0]
    device_ordinal = lax.axis_index("qgrp")
    live_count = filled_supernode_tally[0]
    gather_multiplier = lax.dynamic_slice_in_dim(
        softness_per_channel[0], device_ordinal * local_channel_total, local_channel_total, 0
    ) * per_channel_dimension ** (-0.5)
    queries = (
        jnp.dot(hidden_probe_states, gather_probe_projector, preferred_element_type=jnp.float32)
        .astype(jnp.bfloat16)
        .reshape(latent_rows, local_channel_total, per_channel_dimension)
    )
    key_rows = (
        jnp.dot(supernode_embeddings, gather_lookup_projector, preferred_element_type=jnp.float32)
        .astype(jnp.bfloat16)
        .reshape(slot_count, local_channel_total, per_channel_dimension)
    )
    value_rows = (
        jnp.dot(supernode_embeddings, gather_content_projector, preferred_element_type=jnp.float32)
        .astype(jnp.bfloat16)
        .reshape(slot_count, local_channel_total, per_channel_dimension)
    )
    key_block = math.gcd(slot_count, 512)
    block_count = slot_count // key_block

    def block_scores(block_index):
        offset = block_index * key_block
        is_valid = offset + lax.iota(jnp.int32, key_block) < live_count
        return (masked_scores(queries, key_rows, gather_multiplier, is_valid), is_valid, offset)

    def find_max(block_index, running_max):
        scores, is_valid, offset = block_scores(block_index)
        return jnp.maximum(running_max, jnp.max(scores, axis=-1))

    run_max = lax.fori_loop(
        0,
        block_count,
        find_max,
        jnp.full((latent_rows, local_channel_total), MASKED_SCORE, jnp.float32),
    )

    def accumulate(block_index, running):
        run_sum, run_acc = running
        scores, is_valid, offset = block_scores(block_index)
        weights = jnp.exp(scores - run_max[:, :, None]) * is_valid[None, None, :].astype(
            jnp.float32
        )
        new_sum = run_sum + jnp.sum(weights, axis=-1)
        new_acc = run_acc + jnp.einsum(
            "lhk,khd->lhd",
            weights.astype(jnp.bfloat16),
            value_rows,
            preferred_element_type=jnp.float32,
        )
        return (new_sum, new_acc)

    initial = (
        jnp.zeros((latent_rows, local_channel_total), jnp.float32),
        jnp.zeros((latent_rows, local_channel_total, per_channel_dimension), jnp.float32),
    )
    run_sum, run_acc = lax.fori_loop(0, block_count, accumulate, initial)
    flat_acc = run_acc.reshape(latent_rows, local_channel_total * per_channel_dimension)
    global_max, total_sum, total_acc = combined_all(
        (run_max, run_sum, flat_acc), "cell", combine_partials
    )
    attended = (total_acc / jnp.repeat(total_sum, per_channel_dimension, axis=1)).astype(
        jnp.bfloat16
    )
    partial_value = jnp.dot(attended, gather_final_projector, preferred_element_type=jnp.float32)
    summed = lax.psum(partial_value, "qgrp")
    latent_out = rms_norm(hidden_probe_states.astype(jnp.float32) + summed, hidden_state_gain)
    latent_half = latent_out.astype(jnp.bfloat16)
    unpack_multiplier_uniform = softness_per_channel[1] * per_channel_dimension ** (-0.5)
    half_rows = slot_count // lax.axis_size("qgrp")
    own_begin = device_ordinal * half_rows
    own_tokens = lax.dynamic_slice_in_dim(supernode_embeddings, own_begin, half_rows, 0)
    own_valid = own_begin + lax.iota(jnp.int32, half_rows) < live_count
    local_scale = lax.dynamic_slice_in_dim(
        unpack_multiplier_uniform, device_ordinal * local_channel_total, local_channel_total, 0
    )
    attended_rows = decode_rows(
        supernode_embeddings,
        unpack_probe_projector,
        unpack_lookup_projector,
        unpack_content_projector,
        local_scale,
        latent_half,
        per_channel_dimension,
    )
    update = lax.psum_scatter(
        jnp.dot(attended_rows, unpack_final_projector, preferred_element_type=jnp.float32),
        "qgrp",
        scatter_dimension=0,
        tiled=True,
    )
    tokens_out = jnp.where(
        own_valid[:, None], own_tokens.astype(jnp.float32) + update, jnp.float32(0.0)
    )
    return (latent_out, tokens_out)


def solution(mesh):
    placed = (
        P("cell", None),
        P("cell"),
        P(),
        P(),
        P(None, "qgrp"),
        P(None, "qgrp"),
        P(None, "qgrp"),
        P("qgrp", None),
        P(None, "qgrp"),
        P(None, "qgrp"),
        P(None, "qgrp"),
        P("qgrp", None),
        P(),
    )
    return jax.shard_map(
        body,
        mesh=mesh,
        in_specs=placed,
        out_specs=(P(), P(("cell", "qgrp"), None)),
        check_vma=False,
    )
```

profile of v0, /device:TPU:1, one launch (start us, length us, event | category | flops | bytes accessed | tf_op | source)
XLA Modules:
  0.0 1208.0 jit_solution(8961027397020830862)
XLA Ops:
  12.9 5.8 bitcast_reduce_fusion.1
  19.4 7.3 fusion.9
  27.3 6.4 fusion.12
  35.5 50.9 %all-gather.8.cloned.1.call-done = f32[65536,6]{0,1:T(8,128)} async-done(((f32[1024,6]{0,1:T(8,128)}), f32[65536,6]{0,1:T(8,128)}) %all-gather.8.cloned.1.call-update) | async-done | bytes 1572880 | tf_op jit(solution)/shard_map/all_gather | solution.py:17
  86.4 3.0 slice.39
  89.4 62.8 %all-gather.10.cloned.1.call-done = f32[65536,6]{0,1:T(8,128)} async-done(((f32[1024,6]{0,1:T(8,128)}), f32[65536,6]{0,1:T(8,128)}) %all-gather.10.cloned.1.call-update) | async-done | bytes 1572880 | tf_op jit(solution)/shard_map/all_gather | solution.py:17
  152.2 3.1 slice.40
  155.3 392.8 %all-gather.6.cloned.1.call-done = f32[64,1024,384]{2,1,0:T(8,128)} async-done(((f32[1,1024,384]{2,1,0:T(8,128)}), f32[64,1024,384]{2,1,0:T(8,128)}) %all-gather.6.cloned.1.call-update) | async-done | bytes 100663312 | tf_op jit(solution)/shard_map/all_gather | solution.py:17
  551.2 64.9 %slice.41 = f32[63,1024,384]{2,1,0:T(8,128)} slice(f32[64,1024,384]{2,1,0:T(8,128)} %all-gather.6.cloned.1.call-done), slice={[1:64], [0:1024], [0:384]} | slice | bytes 198180864 | tf_op jit(solution)/shard_map/slice | solution.py:19
  616.2 521.8 %while.2 = (s32[]{:T(128)}, f32[1024,6]{0,1:T(8,128)S(1)}, f32[1024,6]{0,1:T(8,128)S(1)}, f32[1024,384]{0,1:T(8,128)}, f32[63,1024,6]{1,2,0:T(8,128)}, /*index=5...) while((s32[]{:T(128)}, f32[1024,6]{0,1:T(8,128)S(1)}, f32[1024,6]{0,1:T(8,128)S(1)}, ...), condition=%wide.region_3.4_spmd, body=%wide.region_2.3_spmd.sunk | while | flops 1216514 | bytes 11255909 | solution.py:20
  687.8 2.9 fusion.57
  696.1 2.9 fusion.57
  704.4 2.9 fusion.57
  712.6 2.9 fusion.57
  720.9 2.9 fusion.57
  729.2 2.9 fusion.57
  737.5 2.9 fusion.57
  745.8 2.9 fusion.57
  754.0 2.9 fusion.57
  762.3 2.9 fusion.57
  845.1 2.9 fusion.57
  853.4 2.9 fusion.57
  1144.3 27.2 %all-reduce.2.cloned.1.call-done = f32[1024,768]{1,0:T(8,128)} async-done(((f32[1024,768]{1,0:T(8,128)}), f32[1024,768]{1,0:T(8,128)}) %all-reduce.2.cloned.1.call-update) | async-done | bytes 3145744 | tf_op jit(solution)/shard_map/psum | solution.py:186
  1186.2 13.1 %reduce-scatter.2.cloned.1.call-done = f32[256,768]{1,0:T(8,128)} async-done(((f32[512,768]{1,0:T(8,128)}), f32[256,768]{1,0:T(8,128)}) %reduce-scatter.2.cloned.1.call-update) | async-done | bytes 786448 | tf_op jit(solution)/shard_map/reduce_scatter | solution.py:206
  (301 shorter events, 520.3 us)
Async XLA Ops:
  7.2 1132.3 %copy-start = (bf16[384,768]{1,0:T(8,128)(2,1)S(1)}, bf16[384,768]{1,0:T(8,128)(2,1)}, u32[]{:S(2)}) copy-start(bf16[384,768]{1,0:T(8,128)(2,1)} %param.22) | copy-start | bytes 1769476
  7.2 79.2 %all-gather.8.cloned.1.call-start = ((), (), s32[]{:S(2)}) async-start(), calls=%async_computation.4 | async-start | bytes 2129920 | tf_op jit(solution)/shard_map/all_gather | solution.py:17
  19.3 132.9 %all-gather.10.cloned.1.call-start = ((), (), s32[]{:S(2)}) async-start(), calls=%async_computation.5 | async-start | bytes 2129920 | tf_op jit(solution)/shard_map/all_gather | solution.py:17
  19.4 7.4 copy-start.8
  19.4 7.4 copy-start.10
  19.4 7.9 copy-start.7
  26.7 521.3 %all-gather.6.cloned.1.call-start = ((), (), s32[]{:S(2)}) async-start(), calls=%async_computation.1 | async-start | bytes 102236160 | tf_op jit(solution)/shard_map/all_gather | solution.py:17
  35.4 1136.0 %all-reduce.2.cloned.1.call-start = ((), (), s32[]{:S(2)}) async-start(), calls=%async_computation.2 | async-start | bytes 6291456 | tf_op jit(solution)/shard_map/psum | solution.py:186
  551.2 64.9 %slice-start = ((f32[65536,6]{0,1:T(8,128)}), f32[1024,6]{0,1:T(8,128)S(1)}, s32[]{:S(2)}) async-start(f32[65536,6]{0,1:T(8,128)} %all-gather.8.cloned.1.call-done), calls=%async_computation.6 | async-start | bytes 65536 | tf_op jit(solution)/shard_map/slice | solution.py:18
  551.2 64.9 %slice-start.1 = ((f32[65536,6]{0,1:T(8,128)}), f32[1024,6]{0,1:T(8,128)S(1)}, s32[]{:S(2)}) async-start(f32[65536,6]{0,1:T(8,128)} %all-gather.10.cloned.1.call-done), calls=%async_computation.7 | async-start | bytes 65536 | tf_op jit(solution)/shard_map/slice | solution.py:18
  1142.2 29.2 %copy-start.3 = (bf16[1024,768]{1,0:T(8,128)(2,1)S(1)}, bf16[1024,768]{1,0:T(8,128)(2,1)}, u32[]{:S(2)}) copy-start(bf16[1024,768]{1,0:T(8,128)(2,1)} %param.17) | copy-start | bytes 4718596
  1142.2 57.1 %reduce-scatter.2.cloned.1.call-start = ((), (), s32[]{:S(2)}) async-start(), calls=%async_computation.3 | async-start | bytes 2359296 | tf_op jit(solution)/shard_map/reduce_scatter | solution.py:206
  1142.5 31.4 %copy-start.9 = (f32[768]{0:T(1024)S(1)}, f32[768]{0:T(1024)}, u32[]{:S(2)}) copy-start(f32[768]{0:T(1024)} %param.27) | copy-start | bytes 9220
  1171.4 2.8 copy-start.2
  1174.3 1.1 copy-start.4
  1175.3 2.3 copy-start.1
  1175.3 1.5 copy-start.5
  1182.0 2.4 copy-start.6
Sparse Core Ops, SparseCore 0:
  19.4 66.8 all-gather.7
  89.3 62.9 all-gather.9
  155.1 392.9 all-gather.5
  1142.4 29.0 all-reduce.1
  1186.3 12.9 reduce-scatter.1
where the time goes:
time: 1220 us; the launch traced here: 1210 us
  waiting for transfers between devices  547 us (45%)
  local copies, waits for them, and re-layouts  363 us (30%)
  other arithmetic  253 us (21%)
  matrix products  29.3 us (2%)
  between operations  14.7 us (1%)
    all_gather x3, waiting for transfers between devices, combined_all(): pieces = jax.tree.map(lambda part: lax.all_gather(part, axis), value)  507 us
    dynamic_slice x126, local copies, waits for them, and re-layouts, combined_all(): lax.scan(lambda total, piece: (join(total, piece), None), head, tail)  286 us
    add x63, other arithmetic, combine_partials(): left_acc * jnp.repeat(left_factor, per_channel_dimension, axis=1)  184 us
    slice x3, local copies, waits for them, and re-layouts, combined_all(): tail = jax.tree.map(lambda part: part[1:], pieces)  71 us
    add x63, other arithmetic, combine_partials(): both_sum = left_sum * left_factor + right_sum * right_factor  51 us
    psum x1, waiting for transfers between devices, body(): summed = lax.psum(partial_value, 'qgrp')  27.2 us
  transfers between devices with their start and end apart: 5, of which 5 were waited for; matrix products, arithmetic and copies ran while one was open for 2% of the time, Pallas kernels for 0%

commit v1 on v0

v1 whole, which is shorter than its diff:
```python
import functools
import math

import jax
import jax.numpy as jnp
from jax import lax
from jax.experimental import pallas as pl
from jax.experimental.pallas import tpu as pltpu
from jax.sharding import PartitionSpec as P

D = 768
HEADS = 12
HD = 64
MASKED = -1e30
EPS = 1e-06
LOG2E = math.log2(math.e)
MESH = pl.DeviceIdType.MESH
F32 = jnp.float32
BF16 = jnp.bfloat16
VMEM = pl.BlockSpec(memory_space=pltpu.VMEM)
SMEM = pl.BlockSpec(memory_space=pltpu.SMEM)
ANY = pl.BlockSpec(memory_space=pl.ANY)
LIMIT = 60 * 1024 * 1024


def dot(a, b):
    return jnp.dot(a, b, preferred_element_type=F32)


def dot_nt(a, b):
    return lax.dot_general(a, b, (((1,), (1,)), ((), ())), preferred_element_type=F32)


def lanes(shape):
    return lax.broadcasted_iota(jnp.int32, shape, len(shape) - 1)


def three(x):
    high = x.astype(BF16).astype(F32)
    rest = x - high
    middle = rest.astype(BF16).astype(F32)
    return high, middle, rest - middle


def encoder(emb, tally, hidden, soft, wq, wk, wv, out, q_scr, k_scr, v_scr, m_scr, d_scr):
    rows, group = hidden.shape[0], wq.shape[1]
    slots = emb.shape[0]
    pairs = group // 128
    first_head = lax.axis_index("qgrp") * (2 * pairs)
    q_scr[...] = dot(hidden[...], wq[...]).astype(BF16)
    keys = dot(emb[...], wk[...])
    low = lanes((1, group)) % 128 < HD
    k_scr[0] = jnp.where(low, keys, 0.0).astype(BF16)
    k_scr[1] = jnp.where(low, 0.0, keys).astype(BF16)
    values = dot(emb[...], wv[...]).astype(BF16)
    for pair in range(pairs):
        v_scr[pair, :, :128] = values[:, pair * 128 : (pair + 1) * 128]
        v_scr[pair, :, 128:] = jnp.ones((slots, 128), BF16)
    bias = jnp.where(lanes((1, slots)) < tally[0], 0.0, MASKED)
    m_scr[...] = jnp.zeros_like(m_scr)
    d_scr[...] = jnp.zeros_like(d_scr)
    tile = 256

    @pl.loop(0, pairs)
    def _(pair):
        at = pl.ds(pl.multiple_of(pair * 128, 128), 128)
        for start in range(0, rows, tile):
            span = slice(start, start + tile)
            halves = []
            for part in range(2):
                head = 2 * pair + part
                scale = soft[0, first_head + head] * HD**-0.5
                scores = dot_nt(q_scr[span, at], k_scr[part, :, at]) + bias
                top = jnp.max(scores, axis=-1, keepdims=True)
                weights = jnp.exp2((scores - top) * (scale * LOG2E)).astype(BF16)
                halves.append(dot(weights, v_scr[pair]))
                here = lanes((tile, 128)) == head
                m_scr[span, :] = jnp.where(here, top * scale, m_scr[span, :])
                d_scr[span, :] = jnp.where(here, halves[-1][:, 128:], d_scr[span, :])
            mixed = jnp.where(lanes((tile, 128)) < HD, halves[0][:, :128], halves[1][:, :128])
            out[span, at] = mixed.astype(BF16)

    parts = three(m_scr[...]) + three(d_scr[...])
    packed = parts[0]
    for place in range(1, 6):
        packed = packed + pltpu.roll(parts[place], 16 * place, 1)
    out[:, group:] = packed.astype(BF16)


def exchange(
    n,
    msg, hidden, wo, gain, dq, dk, dv, do,
    latents, tq, tk, tv, to,
    inbox, rows_scr, mine, theirs,
    send_sem, recv_sem, pair_send, pair_recv, local_sem, fwd_send, fwd_recv,
):
    cell, core = lax.axis_index("cell"), lax.axis_index("qgrp")
    partner = (cell, 1 - core)
    rows = inbox.shape[1]
    group = wo.shape[0]

    barrier = pltpu.get_barrier_semaphore()

    @pl.loop(1, n)
    def _(step):
        to_cell = lax.rem(cell + step, n)
        pl.semaphore_signal(barrier, inc=1, device_id=(to_cell, core), device_id_type=MESH)

    pl.semaphore_signal(barrier, inc=1, device_id=partner, device_id_type=MESH)
    own = pltpu.make_async_copy(hidden.at[pl.ds(pl.multiple_of(cell * rows, rows), rows)], rows_scr, local_sem.at[0])
    own.start()
    keep = pltpu.make_async_copy(msg.at[cell], inbox.at[cell], local_sem.at[1])
    keep.start()
    pl.semaphore_wait(barrier, n)

    def deal(step):
        to_cell = lax.rem(cell + step, n)
        return pltpu.make_async_remote_copy(
            src_ref=msg.at[to_cell], dst_ref=inbox.at[cell],
            send_sem=send_sem.at[step], recv_sem=recv_sem.at[cell],
            device_id=(to_cell, core), device_id_type=MESH,
        )

    @pl.loop(1, n)
    def _(step):
        deal(step).start()

    weights = [
        pltpu.make_async_remote_copy(
            src_ref=source, dst_ref=target, send_sem=pair_send.at[i], recv_sem=pair_recv.at[i],
            device_id=partner, device_id_type=MESH,
        )
        for i, (source, target) in enumerate(((dq, tq), (dk, tk), (dv, tv), (do, to)))
    ]
    for copy in weights:
        copy.start()
    keep.wait()

    @pl.loop(1, n)
    def _(step):
        source = lax.rem(cell + step, n)
        pltpu.make_async_remote_copy(
            src_ref=msg.at[source], dst_ref=inbox.at[source],
            send_sem=send_sem.at[step], recv_sem=recv_sem.at[source],
            device_id=(source, core), device_id_type=MESH,
        ).wait_recv()

    stats = inbox[:, :, group:].astype(F32).reshape(n * rows, 128)
    top = stats + pltpu.roll(stats, 112, 1) + pltpu.roll(stats, 96, 1)
    total = pltpu.roll(stats, 80, 1) + pltpu.roll(stats, 64, 1) + pltpu.roll(stats, 48, 1)
    used = lanes((n * rows, 128)) < group // HD
    top = jnp.where(used, top, 0.0).reshape(n, rows, 128)
    total = jnp.where(used, total, 0.0).reshape(n, rows, 128)
    factor = jnp.exp(top - jnp.max(top, axis=0, keepdims=True)).astype(BF16)
    total = jnp.sum(factor.astype(F32) * total, axis=0)
    spread = (
        lax.broadcasted_iota(jnp.int32, (128, group), 0) == lanes((128, group)) // HD
    ).astype(BF16)
    wide = dot(factor.reshape(n * rows, 128), spread).reshape(n, rows, group)
    summed = jnp.sum(wide * inbox[:, :, :group].astype(F32), axis=0)
    divisor = sum(dot(part.astype(BF16), spread) for part in three(total))
    attended = (summed / divisor).astype(BF16)
    mine[...] = dot(attended, wo[...])
    swap = pltpu.make_async_remote_copy(
        src_ref=mine, dst_ref=theirs, send_sem=pair_send.at[4], recv_sem=pair_recv.at[4],
        device_id=partner, device_id_type=MESH,
    )
    swap.start()
    own.wait()
    swap.wait()
    before = rows_scr[...].astype(F32) + (mine[...] + theirs[...])
    square = jnp.mean(before * before, axis=-1, keepdims=True)
    latents[cell] = (before * lax.rsqrt(square + EPS) * gain[...]).astype(BF16)

    half = pl.ds(pl.multiple_of(core * group, 128), group)
    other = pl.ds(pl.multiple_of((1 - core) * group, 128), group)

    def share(step):
        to_cell = lax.rem(cell + step, n)
        return pltpu.make_async_remote_copy(
            src_ref=latents.at[cell, :, half], dst_ref=latents.at[cell, :, half],
            send_sem=send_sem.at[n + step], recv_sem=recv_sem.at[n + cell],
            device_id=(to_cell, core), device_id_type=MESH,
        )

    def landed(source):
        return pltpu.make_async_remote_copy(
            src_ref=latents.at[source, :, half], dst_ref=latents.at[source, :, half],
            send_sem=send_sem.at[n], recv_sem=recv_sem.at[n + source],
            device_id=(source, core), device_id_type=MESH,
        )

    def forward(source, part):
        return pltpu.make_async_remote_copy(
            src_ref=latents.at[source, :, part], dst_ref=latents.at[source, :, part],
            send_sem=fwd_send.at[source], recv_sem=fwd_recv.at[source],
            device_id=partner, device_id_type=MESH,
        )

    @pl.loop(1, n)
    def _(step):
        share(step).start()

    @pl.loop(1, n)
    def _(step):
        source = lax.rem(cell + n - step, n)
        landed(source).wait_recv()
        forward(source, half).start()

    @pl.loop(1, n)
    def _(step):
        source = lax.rem(cell + n - step, n)
        forward(source, other).wait_recv()

    @pl.loop(1, n)
    def _(step):
        source = lax.rem(cell + n - step, n)
        forward(source, half).wait_send()
        deal(step).wait_send()
        share(step).wait_send()

    for copy in weights:
        copy.wait()


def decoder(lat, emb, tally, soft, q0, q1, k0, k1, v0, v1, o0, o1, latent_out, tokens, k_scr, v_scr, q_scr, a_scr):
    core = lax.axis_index("qgrp")
    rows, group = lat.shape[0], q0.shape[1]
    slots = tokens.shape[0]
    pairs = group // 128
    own = pl.ds(pl.multiple_of(core * slots, slots), slots)
    latent_out[...] = lat[...].astype(F32)
    low = lanes((1, group)) % 128 < HD
    for side, (wq, wk, wv) in enumerate(((q0, k0, v0), (q1, k1, v1))):
        at = slice(side * group, (side + 1) * group)
        q_scr[:, at] = dot(emb[own, :], wq[...]).astype(BF16)
        keys = dot(lat[...], wk[...])
        k_scr[0, :, at] = jnp.where(low, keys, 0.0).astype(BF16)
        k_scr[1, :, at] = jnp.where(low, 0.0, keys).astype(BF16)
        values = dot(lat[...], wv[...]).astype(BF16)
        for pair in range(pairs):
            v_scr[side * pairs + pair, :, :128] = values[:, pair * 128 : (pair + 1) * 128]
            v_scr[side * pairs + pair, :, 128:] = jnp.ones((rows, 128), BF16)

    @pl.loop(0, 2 * pairs)
    def _(pair):
        at = pl.ds(pl.multiple_of(pair * 128, 128), 128)
        side = lax.rem(core + pair // pairs, 2)
        first = side * (2 * pairs) + 2 * lax.rem(pair, pairs)
        halves = []
        for part in range(2):
            scale = soft[1, first + part] * HD**-0.5
            scores = dot_nt(q_scr[:, at], k_scr[part, :, at])
            top = jnp.max(scores, axis=-1, keepdims=True)
            weights = jnp.exp2((scores - top) * (scale * LOG2E)).astype(BF16)
            mixed = dot(weights, v_scr[pair])
            halves.append(mixed[:, :128] / mixed[:, 128:])
        a_scr[:, at] = jnp.where(lanes((slots, 128)) < HD, halves[0], halves[1]).astype(BF16)

    update = dot(a_scr[:, :group], o0[...]) + dot(a_scr[:, group:], o1[...])
    position = core * slots + lax.broadcasted_iota(jnp.int32, (slots, 1), 0)
    tokens[...] = jnp.where(position < tally[0], emb[own, :].astype(F32) + update, 0.0)


def body(n, emb, tally, hidden, soft, gq, gk, gv, go, uq, uk, uv, uo, gain):
    rows, group = hidden.shape[0], gq.shape[1]
    slots = emb.shape[0]
    pairs = group // 128
    msg = pl.pallas_call(
        encoder,
        name="encoder",
        out_shape=jax.ShapeDtypeStruct((rows, group + 128), BF16),
        in_specs=[VMEM, SMEM, VMEM, SMEM, VMEM, VMEM, VMEM],
        out_specs=VMEM,
        scratch_shapes=[
            pltpu.VMEM((rows, group), BF16),
            pltpu.VMEM((2, slots, group), BF16),
            pltpu.VMEM((pairs, slots, 256), BF16),
            pltpu.VMEM((rows, 128), F32),
            pltpu.VMEM((rows, 128), F32),
        ],
        compiler_params=pltpu.CompilerParams(vmem_limit_bytes=LIMIT),
    )(emb, tally, hidden, soft, gq, gk, gv)
    each = rows // n
    dma = pltpu.SemaphoreType.DMA
    like = lambda x: jax.ShapeDtypeStruct(x.shape, x.dtype)
    latents, tq, tk, tv, to = pl.pallas_call(
        functools.partial(exchange, n),
        name="exchange",
        out_shape=(jax.ShapeDtypeStruct((n, each, D), BF16), like(uq), like(uk), like(uv), like(uo)),
        in_specs=[VMEM, ANY, VMEM, VMEM, ANY, ANY, ANY, ANY],
        out_specs=(VMEM, ANY, ANY, ANY, ANY),
        scratch_shapes=[
            pltpu.VMEM((n, each, group + 128), BF16),
            pltpu.VMEM((each, D), BF16),
            pltpu.VMEM((each, D), F32),
            pltpu.VMEM((each, D), F32),
            dma((2 * n,)), dma((2 * n,)), dma((5,)), dma((5,)), dma((2,)), dma((n,)), dma((n,)),
        ],
        compiler_params=pltpu.CompilerParams(collective_id=0, has_side_effects=True, vmem_limit_bytes=LIMIT),
    )(msg.reshape(n, each, group + 128), hidden, go, gain.reshape(1, D), uq, uk, uv, uo)
    half = slots // 2
    return pl.pallas_call(
        decoder,
        name="decoder",
        out_shape=(jax.ShapeDtypeStruct((rows, D), F32), jax.ShapeDtypeStruct((half, D), F32)),
        in_specs=[VMEM, VMEM, SMEM, SMEM] + [VMEM] * 8,
        out_specs=(VMEM, VMEM),
        scratch_shapes=[
            pltpu.VMEM((2, rows, D), BF16),
            pltpu.VMEM((2 * pairs, rows, 256), BF16),
            pltpu.VMEM((half, D), BF16),
            pltpu.VMEM((half, D), BF16),
        ],
        compiler_params=pltpu.CompilerParams(vmem_limit_bytes=LIMIT),
    )(latents.reshape(rows, D), emb, tally, soft, uq, tq, uk, tk, uv, tv, uo, to)


def solution(mesh):
    column, row = P(None, "qgrp"), P("qgrp", None)
    placed = (P("cell", None), P("cell"), P(), P(), column, column, column, row, column, column, column, row, P())
    return jax.shard_map(
        functools.partial(body, mesh.shape["cell"]),
        mesh=mesh,
        in_specs=placed,
        out_specs=(P(), P(("cell", "qgrp"), None)),
        check_vma=False,
    )
```

time: 1220 us -> 79.2 us (0.06)
  waiting for transfers between devices: 547 us -> 0 us
  local copies, waits for them, and re-layouts: 363 us -> 1.27 us
  other arithmetic: 253 us -> 0 us
  Pallas kernels: 0 us -> 76.4 us
  matrix products: 29.3 us -> 0 us
  between operations: 14.7 us -> 1.29 us
    all_gather x3 -> x0, waiting for transfers between devices: 507 us -> none  [combined_all(): pieces = jax.tree.map(lambda part: lax.all_gather(part, axis), value)]
    dynamic_slice x127 -> x0, local copies, waits for them, and re-layouts: 286 us -> none  [the longest x126 286 us: combined_all(): lax.scan(lambda total, piece: (join(total, piece), None), head, tail)]
    add x126 -> x0, other arithmetic: 235 us -> none  [the longest x63 184 us: combine_partials(): left_acc * jnp.repeat(left_factor, per_channel_dimension, axis=1)]
    pallas_call x0 -> x3, Pallas kernels: none -> 76.4 us  [the longest x1 49.8 us: body(): pl.pallas_call(functools.partial(exchange, n), name='exchange', out_shape...]
    slice x7 -> x0, local copies, waits for them, and re-layouts: 71 us -> none  [the longest x3 71 us: combined_all(): tail = jax.tree.map(lambda part: part[1:], pieces)]
    dot_general x12 -> x0, matrix products: 29.3 us -> none  [the longest x1 6.44 us: accumulate(): jnp.einsum('lhk,khd->lhd', weights.astype(jnp.bfloat16), value_rows, pref...]
    psum x1 -> x0, waiting for transfers between devices: 27.2 us -> none  [body(): summed = lax.psum(partial_value, 'qgrp')]
    reduce_scatter x1 -> x0, waiting for transfers between devices: 13.1 us -> none  [body(): lax.psum_scatter(jnp.dot(attended_rows, unpack_final_projector, preferred...]
  transfers between devices with their start and end apart: 5 -> 0, of which waited for: 5 -> 0; matrix products, arithmetic and copies ran while one was open for 2% -> 0% of each run, Pallas kernels for 0% -> 0%
where the time goes in v1:
time: 79.2 us; the launch traced here: 79 us
  Pallas kernels  76.4 us (96%)
  between operations  1.29 us (2%)
  local copies, waits for them, and re-layouts  1.27 us (2%)
    pallas_call x1, Pallas kernels, body(): pl.pallas_call(functools.partial(exchange, n), name='exchange', out_shape...  49.8 us
    pallas_call x1, Pallas kernels, body(): pl.pallas_call(decoder, name='decoder', out_shape=(jax.ShapeDtypeStruct((...  16 us
    pallas_call x1, Pallas kernels, body(): pl.pallas_call(encoder, name='encoder', out_shape=jax.ShapeDtypeStruct((r...  10.6 us

profile of v1, /device:TPU:1, one launch (start us, length us, event | category | flops | bytes accessed | tf_op | source)
XLA Modules:
  0.0 79.0 jit_solution(1969773034815054900)
XLA Ops:
  1.3 1.3 %reshape.14.gain = f32[1,768]{1,0:T(1,128)} reshape(f32[768]{0:T(1024)} %param.25) | data formatting | bytes 6144 | tf_op jit(solution)/shard_map/reshape | solution.py:301
  2.5 10.6 %encoder.1 = bf16[1024,512]{1,0:T(8,128)(2,1)} custom-call(bf16[512,768]{1,0:T(8,128)(2,1)} %emb.3, s32[1]{0:T(128)S(6)} %copy.15.tally, bf16[1024,768]{1,0:T(8,128)(2,1)} %hidden.3, f32[2,12]{1,0:T(2,128)} %soft.3, bf16[768,384]{1,0:T(8,128)(2,1)} %wq.1, bf16[768,384]{1,0:T(8,128)(2,1)} %wk.1, bf16[768,384]{1,0:T(8,128)(2,1)} %wv.1), custom_call_target="tpu_custom_call" | custom-call | tf_op jit(solution)/shard_map/encoder/pallas_call | solution.py:269
  13.1 49.8 %exchange.1 = (bf16[64,16,768]{2,1,0:T(8,128)(2,1)}, bf16[768,384]{1,0:T(8,128)(2,1)}, bf16[768,384]{1,0:T(8,128)(2,1)}, bf16[768,384]{1,0:T(8,128)(2,1)}, bf16[384,768]{1,0:T(8,128)(2,1)}) custom-call(bf16[64,16,512]{2,1,0:T(8,128)(2,1)} %bitcast.2, bf16[1024,768]{1,0:T(8,128)(2,1)} %hidden.3, bf16[384,768]{1,0:T(8,128)(2,1)} %wo.1, ...), custom_call_target="tpu_custom_call" | custom-call | tf_op jit(solution)/shard_map/exchange/pallas_call | solution.py:287
  63.0 16.0 %decoder.1 = (f32[1024,768]{1,0:T(8,128)}, f32[256,768]{1,0:T(8,128)}) custom-call(bf16[1024,768]{1,0:T(8,128)(2,1)} %bitcast.3, bf16[512,768]{1,0:T(8,128)(2,1)} %emb.3, s32[1]{0:T(128)S(6)} %copy.15.tally, f32[2,12]{1,0:T(2,128)} %soft.3, bf16[768,384]{1,0:T(8,128)(2,1)} %q0.1, bf16[768,384]{1,0:T(8,128)(2,1)} %get-tuple-element.8.q1, ...), custom_call_target="tpu_custom_call" | custom-call | tf_op jit(solution)/shard_map/decoder/pallas_call | solution.py:303

commit v2 on v1

v2 whole, which is shorter than its diff:
```python
import functools
import math

import jax
import jax.numpy as jnp
from jax import lax
from jax.experimental import pallas as pl
from jax.experimental.pallas import tpu as pltpu
from jax.sharding import PartitionSpec as P

D = 768
HEADS = 12
HD = 64
RING = 4
COLOURS = 3
REDUCE_AXES = ((0, 1, 2), (1, 2, 0), (2, 0, 1))
GATHER_AXES = ((2, 1, 0), (0, 2, 1), (1, 0, 2))
MASKED = -1e30
EPS = 1e-06
LOG2E = math.log2(math.e)
MESH = pl.DeviceIdType.MESH
F32 = jnp.float32
BF16 = jnp.bfloat16
VMEM = pl.BlockSpec(memory_space=pltpu.VMEM)
SMEM = pl.BlockSpec(memory_space=pltpu.SMEM)
ANY = pl.BlockSpec(memory_space=pl.ANY)
LIMIT = 60 * 1024 * 1024


def dot(a, b):
    return jnp.dot(a, b, preferred_element_type=F32)


def dot_nt(a, b):
    return lax.dot_general(a, b, (((1,), (1,)), ((), ())), preferred_element_type=F32)


def lanes(shape):
    return lax.broadcasted_iota(jnp.int32, shape, len(shape) - 1)


def three(x):
    high = x.astype(BF16).astype(F32)
    rest = x - high
    middle = rest.astype(BF16).astype(F32)
    return high, middle, rest - middle


def packed_stats(top, total):
    place = lanes(top.shape) % HD
    packed = jnp.zeros_like(top)
    for i, part in enumerate(three(top) + three(total)):
        packed = jnp.where(place == i, part, packed)
    return packed.astype(BF16)


def unpacking():
    source = lax.broadcasted_iota(jnp.int32, (128, 256), 0)
    target = lanes((128, 256))
    same = (target % 128) // HD == source // HD
    return (same & ((source % HD) // 3 == target // 128)).astype(BF16)


def merged(box):
    count, rows, _ = box.shape
    stats = dot(box[:, :, 128:].reshape(count * rows, 128), unpacking()).reshape(count, rows, 256)
    top, total = stats[:, :, :128], stats[:, :, 128:]
    best = jnp.max(top, axis=0)
    factor = jnp.exp(top - best)
    return jnp.sum(factor * box[:, :, :128].astype(F32), axis=0), best, jnp.sum(factor * total, axis=0)


def gather(
    emb, tally, hidden, soft, wq, wk, wv, wo, gain, dq, dk, dv, do,
    latents, tq, tk, tv, to,
    q_scr, k_scr, v_scr, out1, box1, out2, box2, out3, box3, mine, theirs,
    red_send, red_recv, gat_send, gat_recv, fwd_send, fwd_recv, pair_send, pair_recv,
):
    cell, core = lax.axis_index("cell"), lax.axis_index("qgrp")
    here = (cell // 16, (cell // 4) % 4, cell % 4)
    partner = (cell, 1 - core)
    rows, group = hidden.shape[0], wq.shape[1]
    slots = emb.shape[0]
    quarter, each = rows // RING, rows // RING**3

    def peer(axis, digit):
        at = [digit if i == axis else here[i] for i in range(3)]
        return ((at[0] * RING + at[1]) * RING + at[2], core)

    def turn(axis, step):
        return lax.rem(here[axis] + step, RING)

    barrier = pltpu.get_barrier_semaphore()
    for axis in range(3):
        for step in range(1, RING):
            pl.semaphore_signal(barrier, inc=1, device_id=peer(axis, turn(axis, step)), device_id_type=MESH)
    pl.semaphore_signal(barrier, inc=1, device_id=partner, device_id_type=MESH)

    queries = dot(hidden[...], wq[...]).astype(BF16)
    keys = dot(emb[...], wk[...])
    low = lanes((1, group)) % 128 < HD
    k_scr[0] = jnp.where(low, keys, 0.0).astype(BF16)
    k_scr[1] = jnp.where(low, 0.0, keys).astype(BF16)
    values = dot(emb[...], wv[...]).astype(BF16)
    for pair in range(COLOURS):
        block = slice(pair * 128, (pair + 1) * 128)
        q_scr[pair] = queries[:, block].reshape(RING, RING, RING, each, 128)
        v_scr[pair, :, :128] = values[:, block]
        v_scr[pair, :, 128:] = jnp.ones((slots, 128), BF16)
    bias = jnp.where(lanes((1, slots)) < tally[0], 0.0, MASKED)
    first_head = core * (2 * COLOURS)

    pl.semaphore_wait(barrier, 10)
    weights = [
        pltpu.make_async_remote_copy(
            src_ref=source, dst_ref=target, send_sem=pair_send.at[i], recv_sem=pair_recv.at[i],
            device_id=partner, device_id_type=MESH,
        )
        for i, (source, target) in enumerate(((dq, tq), (dk, tk), (dv, tv), (do, to)))
    ]
    for copy in weights:
        copy.start()

    def tile(pair, digit):
        axis = REDUCE_AXES[pair][0]
        q = q_scr[(pair,) + tuple(digit if i == axis else slice(None) for i in range(axis + 1))]
        q = q.reshape(quarter, 128)
        first = lanes((quarter, 128)) < HD
        tops, halves = [], []
        for part in range(2):
            scale = soft[0, first_head + 2 * pair + part] * HD**-0.5
            scores = dot_nt(q, k_scr[part, :, pair * 128 : (pair + 1) * 128]) + bias
            top = jnp.max(scores, axis=-1, keepdims=True)
            weight = jnp.exp2((scores - top) * (scale * LOG2E)).astype(BF16)
            halves.append(dot(weight, v_scr[pair]))
            tops.append(top * scale)
        mixed = jnp.where(first, halves[0][:, :128], halves[1][:, :128])
        total = jnp.where(first, halves[0][:, 128:], halves[1][:, 128:])
        return mixed.astype(BF16), packed_stats(jnp.where(first, tops[0], tops[1]), total)

    outs, boxes = (out1, out2, out3), (box1, box2, box3)

    def reduce_copy(stage, pair, digit):
        axis = REDUCE_AXES[pair][stage]
        return pltpu.make_async_remote_copy(
            src_ref=outs[stage].at[pair, digit], dst_ref=boxes[stage].at[pair, here[axis]],
            send_sem=red_send.at[stage, pair, digit], recv_sem=red_recv.at[stage, pair, here[axis]],
            device_id=peer(axis, digit), device_id_type=MESH,
        )

    def reduce_arrived(stage, pair, digit):
        axis = REDUCE_AXES[pair][stage]
        pltpu.make_async_remote_copy(
            src_ref=outs[stage].at[pair, digit], dst_ref=boxes[stage].at[pair, digit],
            send_sem=red_send.at[stage, pair, digit], recv_sem=red_recv.at[stage, pair, digit],
            device_id=peer(axis, digit), device_id_type=MESH,
        ).wait_recv()

    @pl.loop(1, RING)
    def _(step):
        for pair in range(COLOURS):
            digit = turn(REDUCE_AXES[pair][0], step)
            mixed, stats = tile(pair, digit)
            out1[pair, digit, :, :128] = mixed
            out1[pair, digit, :, 128:] = stats
            reduce_copy(0, pair, digit).start()

    for pair in range(COLOURS):
        own = here[REDUCE_AXES[pair][0]]
        mixed, stats = tile(pair, own)
        box1[pair, own, :, :128] = mixed
        box1[pair, own, :, 128:] = stats

    for stage in (1, 2):
        for pair in range(COLOURS):
            for step in range(1, RING):
                reduce_arrived(stage - 1, pair, turn(REDUCE_AXES[pair][stage - 1], step))
            acc, top, total = merged(boxes[stage - 1][pair])
            joined = jnp.concatenate([acc.astype(BF16), packed_stats(top, total)], axis=1)
            axis = REDUCE_AXES[pair][stage]
            if stage == 1:
                joined = joined.reshape(RING, RING, each, 256)
                rest = [i for i in range(3) if i != REDUCE_AXES[pair][0]]
                pieces = [
                    (joined[i] if rest[0] == axis else joined[:, i]).reshape(RING * each, 256)
                    for i in range(RING)
                ]
            else:
                pieces = [joined[i * each : (i + 1) * each] for i in range(RING)]
            for i in range(RING):
                outs[stage][pair, i] = pieces[i]
            boxes[stage][pair, here[axis]] = outs[stage][pair, here[axis]]
            for step in range(1, RING):
                reduce_copy(stage, pair, turn(axis, step)).start()

    partial = jnp.zeros((each, D), F32)
    for pair in range(COLOURS):
        for step in range(1, RING):
            reduce_arrived(2, pair, turn(REDUCE_AXES[pair][2], step))
        acc, _, total = merged(box3[pair])
        partial += dot((acc / total).astype(BF16), wo[pair * 128 : (pair + 1) * 128, :])
    mine[...] = partial
    swap = pltpu.make_async_remote_copy(
        src_ref=mine, dst_ref=theirs, send_sem=pair_send.at[4], recv_sem=pair_recv.at[4],
        device_id=partner, device_id_type=MESH,
    )
    swap.start()
    swap.wait()
    before = hidden[pl.ds(pl.multiple_of(cell * each, each), each), :].astype(F32) + (mine[...] + theirs[...])
    square = jnp.mean(before * before, axis=-1, keepdims=True)
    normal = (before * lax.rsqrt(square + EPS) * gain[...].reshape(1, D)).astype(BF16)
    for colour in range(COLOURS):
        block = normal[:, colour * 256 : (colour + 1) * 256]
        latents[2 * colour + core, here[0], here[1], here[2]] = jnp.where(core == 0, block[:, :128], block[:, 128:])

    def slab(colour, side, stage, axis=None, digit=None):
        known = GATHER_AXES[colour][stage:]
        at = [here[i] if i in known else slice(None) for i in range(3)]
        if axis is not None:
            at[axis] = digit
        return latents.at[(2 * colour + side,) + tuple(at)]

    def gather_copy(stage, colour, digit):
        axis = GATHER_AXES[colour][stage]
        return pltpu.make_async_remote_copy(
            src_ref=slab(colour, core, stage), dst_ref=slab(colour, core, stage),
            send_sem=gat_send.at[stage, colour, digit], recv_sem=gat_recv.at[stage, colour, here[axis]],
            device_id=peer(axis, digit), device_id_type=MESH,
        )

    def gather_arrived(stage, colour, digit):
        axis = GATHER_AXES[colour][stage]
        pltpu.make_async_remote_copy(
            src_ref=slab(colour, core, stage), dst_ref=slab(colour, core, stage, axis, digit),
            send_sem=gat_send.at[stage, colour, digit], recv_sem=gat_recv.at[stage, colour, digit],
            device_id=peer(axis, digit), device_id_type=MESH,
        ).wait_recv()

    def forward(colour, side, digit):
        axis = GATHER_AXES[colour][2]
        part = slab(colour, side, 2, axis, digit)
        return pltpu.make_async_remote_copy(
            src_ref=part, dst_ref=part, send_sem=fwd_send.at[colour, digit], recv_sem=fwd_recv.at[colour, digit],
            device_id=partner, device_id_type=MESH,
        )

    for stage in range(3):
        for colour in range(COLOURS):
            if stage:
                for step in range(1, RING):
                    gather_arrived(stage - 1, colour, turn(GATHER_AXES[colour][stage - 1], step))
            axis = GATHER_AXES[colour][stage]
            for step in range(1, RING):
                gather_copy(stage, colour, turn(axis, step)).start()
            if stage == 2:
                forward(colour, core, here[axis]).start()
    for step in (1, 3, 2):
        for colour in range(COLOURS):
            digit = turn(GATHER_AXES[colour][2], step)
            gather_arrived(2, colour, digit)
            forward(colour, core, digit).start()
    for colour in range(COLOURS):
        for digit in range(RING):
            forward(colour, 1 - core, digit).wait_recv()
    for colour in range(COLOURS):
        for digit in range(RING):
            forward(colour, core, digit).wait_send()
        for stage in range(3):
            for step in range(1, RING):
                reduce_copy(stage, colour, turn(REDUCE_AXES[colour][stage], step)).wait_send()
                gather_copy(stage, colour, turn(GATHER_AXES[colour][stage], step)).wait_send()
    for copy in weights:
        copy.wait()


def decoder(lat, emb, tally, soft, q0, q1, k0, k1, v0, v1, o0, o1, latent_out, tokens, k_scr, v_scr, q_scr, a_scr):
    core = lax.axis_index("qgrp")
    blocks, rows, _ = lat.shape
    group = q0.shape[1]
    slots = tokens.shape[0]
    pairs = group // 128
    own = pl.ds(pl.multiple_of(core * slots, slots), slots)
    latent = jnp.concatenate([lat[i] for i in range(blocks)], axis=1)
    latent_out[...] = latent.astype(F32)
    low = lanes((1, group)) % 128 < HD
    for side, (wq, wk, wv) in enumerate(((q0, k0, v0), (q1, k1, v1))):
        at = slice(side * group, (side + 1) * group)
        q_scr[:, at] = dot(emb[own, :], wq[...]).astype(BF16)
        keys = dot(latent, wk[...])
        k_scr[0, :, at] = jnp.where(low, keys, 0.0).astype(BF16)
        k_scr[1, :, at] = jnp.where(low, 0.0, keys).astype(BF16)
        values = dot(latent, wv[...]).astype(BF16)
        for pair in range(pairs):
            v_scr[side * pairs + pair, :, :128] = values[:, pair * 128 : (pair + 1) * 128]
            v_scr[side * pairs + pair, :, 128:] = jnp.ones((rows, 128), BF16)

    @pl.loop(0, 2 * pairs)
    def _(pair):
        at = pl.ds(pl.multiple_of(pair * 128, 128), 128)
        side = lax.rem(core + pair // pairs, 2)
        first = side * (2 * pairs) + 2 * lax.rem(pair, pairs)
        halves = []
        for part in range(2):
            scale = soft[1, first + part] * HD**-0.5
            scores = dot_nt(q_scr[:, at], k_scr[part, :, at])
            top = jnp.max(scores, axis=-1, keepdims=True)
            weights = jnp.exp2((scores - top) * (scale * LOG2E)).astype(BF16)
            mixed = dot(weights, v_scr[pair])
            halves.append(mixed[:, :128] / mixed[:, 128:])
        a_scr[:, at] = jnp.where(lanes((slots, 128)) < HD, halves[0], halves[1]).astype(BF16)

    update = dot(a_scr[:, :group], o0[...]) + dot(a_scr[:, group:], o1[...])
    position = core * slots + lax.broadcasted_iota(jnp.int32, (slots, 1), 0)
    tokens[...] = jnp.where(position < tally[0], emb[own, :].astype(F32) + update, 0.0)


def body(emb, tally, hidden, soft, gq, gk, gv, go, uq, uk, uv, uo, gain):
    rows, group = hidden.shape[0], gq.shape[1]
    slots = emb.shape[0]
    each = rows // RING**3
    dma = pltpu.SemaphoreType.DMA
    like = lambda x: jax.ShapeDtypeStruct(x.shape, x.dtype)
    boxes = []
    for part in (rows // RING, rows // RING**2, each):
        boxes += [pltpu.VMEM((COLOURS, RING, part, 256), BF16)] * 2
    latents, tq, tk, tv, to = pl.pallas_call(
        gather,
        name="gather",
        out_shape=(
            jax.ShapeDtypeStruct((2 * COLOURS, RING, RING, RING, each, 128), BF16),
            like(uq), like(uk), like(uv), like(uo),
        ),
        in_specs=[VMEM, SMEM, VMEM, SMEM, VMEM, VMEM, VMEM, VMEM, VMEM, ANY, ANY, ANY, ANY],
        out_specs=(VMEM, ANY, ANY, ANY, ANY),
        scratch_shapes=[
            pltpu.VMEM((COLOURS, RING, RING, RING, each, 128), BF16),
            pltpu.VMEM((2, slots, group), BF16),
            pltpu.VMEM((COLOURS, slots, 256), BF16),
            *boxes,
            pltpu.VMEM((each, D), F32),
            pltpu.VMEM((each, D), F32),
            dma((3, COLOURS, RING)), dma((3, COLOURS, RING)),
            dma((3, COLOURS, RING)), dma((3, COLOURS, RING)),
            dma((COLOURS, RING)), dma((COLOURS, RING)), dma((5,)), dma((5,)),
        ],
        compiler_params=pltpu.CompilerParams(collective_id=0, has_side_effects=True, vmem_limit_bytes=LIMIT),
    )(emb, tally, hidden, soft, gq, gk, gv, go, gain, uq, uk, uv, uo)
    half = slots // 2
    return pl.pallas_call(
        decoder,
        name="decoder",
        out_shape=(jax.ShapeDtypeStruct((rows, D), F32), jax.ShapeDtypeStruct((half, D), F32)),
        in_specs=[VMEM, VMEM, SMEM, SMEM] + [VMEM] * 8,
        out_specs=(VMEM, VMEM),
        scratch_shapes=[
            pltpu.VMEM((2, rows, D), BF16),
            pltpu.VMEM((2 * COLOURS, rows, 256), BF16),
            pltpu.VMEM((half, D), BF16),
            pltpu.VMEM((half, D), BF16),
        ],
        compiler_params=pltpu.CompilerParams(vmem_limit_bytes=LIMIT),
    )(latents.reshape(2 * COLOURS, rows, 128), emb, tally, soft, uq, tq, uk, tk, uv, tv, uo, to)


def solution(mesh):
    column, row = P(None, "qgrp"), P("qgrp", None)
    placed = (P("cell", None), P("cell"), P(), P(), column, column, column, row, column, column, column, row, P())
    return jax.shard_map(
        body,
        mesh=mesh,
        in_specs=placed,
        out_specs=(P(), P(("cell", "qgrp"), None)),
        check_vma=False,
    )
```

time: 79.2 us -> 65.2 us (0.82)
  Pallas kernels: 76.4 us -> 63.7 us
  local copies, waits for them, and re-layouts: 1.27 us -> 0 us
    pallas_call x2 -> x1, Pallas kernels: 60.4 us -> 47.9 us  [body(): pl.pallas_call(gather, name='gather', out_shape=(jax.ShapeDtypeStruct((2...]
    reshape x1 -> x0, local copies, waits for them, and re-layouts: 1.27 us -> none  [body(): gain.reshape(1, D)]
where the time goes in v2:
time: 65.2 us; the launch traced here: 65 us
  Pallas kernels  63.7 us (98%)
  between operations  1.29 us (2%)
    pallas_call x1, Pallas kernels, body(): pl.pallas_call(gather, name='gather', out_shape=(jax.ShapeDtypeStruct((2...  47.9 us
    pallas_call x1, Pallas kernels, body(): pl.pallas_call(decoder, name='decoder', out_shape=(jax.ShapeDtypeStruct((...  15.9 us

profile of v2, /device:TPU:1, one launch (start us, length us, event | category | flops | bytes accessed | tf_op | source)
XLA Modules:
  0.0 65.0 jit_solution(7578603287200075334)
XLA Ops:
  1.3 47.9 %gather.1 = (bf16[6,4,4,4,16,128]{5,4,3,2,1,0:T(8,128)(2,1)}, bf16[768,384]{1,0:T(8,128)(2,1)}, bf16[768,384]{1,0:T(8,128)(2,1)}, bf16[768,384]{1,0:T(8,128)(2,1)}, bf16[384,768]{1,0:T(8,128)(2,1)}) custom-call(bf16[512,768]{1,0:T(8,128)(2,1)} %emb.3, s32[1]{0:T(128)S(6)} %copy.15.tally, bf16[1024,768]{1,0:T(8,128)(2,1)} %hidden.1, f32[2,12]{1,0:T(2,128)} %soft.3, ...), custom_call_target="tpu_custom_call" | custom-call | tf_op jit(solution)/shard_map/gather/pallas_call | solution.py:326
  49.2 15.9 %decoder.1 = (f32[1024,768]{1,0:T(8,128)}, f32[256,768]{1,0:T(8,128)}) custom-call(bf16[6,1024,128]{2,1,0:T(8,128)(2,1)} %bitcast.1, bf16[512,768]{1,0:T(8,128)(2,1)} %emb.3, s32[1]{0:T(128)S(6)} %copy.15.tally, f32[2,12]{1,0:T(2,128)} %soft.3, bf16[768,384]{1,0:T(8,128)(2,1)} %q0.1, bf16[768,384]{1,0:T(8,128)(2,1)} %get-tuple-element.8.q1, ...), custom_call_target="tpu_custom_call" | custom-call | tf_op jit(solution)/shard_map/decoder/pallas_call | solution.py:349

commit v3 on v2

--- a/solution.py
+++ b/solution.py
@@ -23,8 +23,8 @@
 BF16 = jnp.bfloat16
 VMEM = pl.BlockSpec(memory_space=pltpu.VMEM)
 SMEM = pl.BlockSpec(memory_space=pltpu.SMEM)
-ANY = pl.BlockSpec(memory_space=pl.ANY)
-LIMIT = 60 * 1024 * 1024
+HBM = pl.BlockSpec(memory_space=pltpu.HBM)
+LIMIT = 36 * 1024 * 1024
 
 
 def dot(a, b):
@@ -70,11 +70,30 @@
     return jnp.sum(factor * box[:, :, :128].astype(F32), axis=0), best, jnp.sum(factor * total, axis=0)
 
 
+def attend(q, k, v, scales):
+    first = lanes((1, 128)) < HD
+    zero = jnp.zeros_like(k)
+    halves = (jnp.where(first, k, zero), jnp.where(first, zero, k))
+    widened = jnp.concatenate([v, jnp.ones_like(v)], axis=1)
+    tile, results = 128, []
+    for start in range(0, q.shape[0], tile):
+        mixed = []
+        for key, scale in zip(halves, scales):
+            scores = dot_nt(q[start : start + tile], key)
+            top = jnp.max(scores, axis=-1, keepdims=True)
+            weight = jnp.exp2((scores - top) * (scale * LOG2E)).astype(BF16)
+            both = dot(weight, widened)
+            mixed.append(both[:, :128] / both[:, 128:])
+        results.append(jnp.where(first, mixed[0], mixed[1]).astype(BF16))
+    return jnp.concatenate(results, axis=0)
+
+
 def gather(
-    emb, tally, hidden, soft, wq, wk, wv, wo, gain, dq, dk, dv, do,
-    latents, tq, tk, tv, to,
+    emb_h, tally, hidden_h, soft_h, wq_h, wk_h, wv_h, wo_h, gain_h, dq_h, dk_h, dv_h, do_h,
+    latents, att, q_other, k_other, v_other, o_other,
+    emb, hidden, soft, wq, wk, wv, wo, gain, dq, dk, dv, dq_other, q_own, k_own, v_own,
     q_scr, k_scr, v_scr, out1, box1, out2, box2, out3, box3, mine, theirs,
-    red_send, red_recv, gat_send, gat_recv, fwd_send, fwd_recv, pair_send, pair_recv,
+    load_sem, red_send, red_recv, gat_send, gat_recv, fwd_send, fwd_recv, pair_send, pair_recv,
 ):
     cell, core = lax.axis_index("cell"), lax.axis_index("qgrp")
     here = (cell // 16, (cell // 4) % 4, cell % 4)
@@ -82,6 +101,18 @@
     rows, group = hidden.shape[0], wq.shape[1]
     slots = emb.shape[0]
     quarter, each = rows // RING, rows // RING**3
+    loads = {}
+    for i, (name, source, target) in enumerate((
+        ("emb", emb_h, emb), ("wk", wk_h, wk), ("wv", wv_h, wv), ("hidden", hidden_h, hidden), ("wq", wq_h, wq),
+        ("soft", soft_h, soft), ("dq", dq_h, dq), ("wo", wo_h, wo), ("gain", gain_h, gain),
+        ("dk", dk_h, dk), ("dv", dv_h, dv),
+    )):
+        loads[name] = pltpu.make_async_copy(source, target, load_sem.at[i])
+        loads[name].start()
+
+    def ready(*names):
+        for name in names:
+            loads[name].wait()
 
     def peer(axis, digit):
         at = [digit if i == axis else here[i] for i in range(3)]
@@ -89,6 +120,12 @@
 
     def turn(axis, step):
         return lax.rem(here[axis] + step, RING)
+
+    def to_partner(i, source, target):
+        return pltpu.make_async_remote_copy(
+            src_ref=source, dst_ref=target, send_sem=pair_send.at[i], recv_sem=pair_recv.at[i],
+            device_id=partner, device_id_type=MESH,
+        )
 
     barrier = pltpu.get_barrier_semaphore()
     for axis in range(3):
@@ -96,29 +133,27 @@
             pl.semaphore_signal(barrier, inc=1, device_id=peer(axis, turn(axis, step)), device_id_type=MESH)
     pl.semaphore_signal(barrier, inc=1, device_id=partner, device_id_type=MESH)
 
-    queries = dot(hidden[...], wq[...]).astype(BF16)
+    ready("emb", "wk")
     keys = dot(emb[...], wk[...])
     low = lanes((1, group)) % 128 < HD
     k_scr[0] = jnp.where(low, keys, 0.0).astype(BF16)
     k_scr[1] = jnp.where(low, 0.0, keys).astype(BF16)
+    ready("wv")
     values = dot(emb[...], wv[...]).astype(BF16)
     for pair in range(COLOURS):
-        block = slice(pair * 128, (pair + 1) * 128)
-        q_scr[pair] = queries[:, block].reshape(RING, RING, RING, each, 128)
-        v_scr[pair, :, :128] = values[:, block]
+        v_scr[pair, :, :128] = values[:, pair * 128 : (pair + 1) * 128]
         v_scr[pair, :, 128:] = jnp.ones((slots, 128), BF16)
+    ready("hidden", "wq")
+    queries = dot(hidden[...], wq[...]).astype(BF16)
+    for pair in range(COLOURS):
+        q_scr[pair] = queries[:, pair * 128 : (pair + 1) * 128].reshape(RING, RING, RING, each, 128)
     bias = jnp.where(lanes((1, slots)) < tally[0], 0.0, MASKED)
     first_head = core * (2 * COLOURS)
+    ready("soft")
 
     pl.semaphore_wait(barrier, 10)
-    weights = [
-        pltpu.make_async_remote_copy(
-            src_ref=source, dst_ref=target, send_sem=pair_send.at[i], recv_sem=pair_recv.at[i],
-            device_id=partner, device_id_type=MESH,
-        )
-        for i, (source, target) in enumerate(((dq, tq), (dk, tk), (dv, tv), (do, to)))
-    ]
-    for copy in weights:
+    swaps = [to_partner(0, dq_h, dq_other), to_partner(1, do_h, o_other)]
+    for copy in swaps:
         copy.start()
 
     def tile(pair, digit):
@@ -170,6 +205,17 @@
         mixed, stats = tile(pair, own)
         box1[pair, own, :, :128] = mixed
         box1[pair, own, :, 128:] = stats
+
+    half = slots // 2
+    ready("dq", "wo", "gain", "dk", "dv")
+    mine_rows = emb[pl.ds(pl.multiple_of(core * half, half), half), :]
+    for target, weight in ((q_own, dq), (q_other, dq_other)):
+        if weight is dq_other:
+            for copy in swaps:
+                copy.wait()
+        projected = dot(mine_rows, weight[...]).astype(BF16)
+        for pair in range(COLOURS):
+            target[pair] = projected[:, pair * 128 : (pair + 1) * 128]
 
     for stage in (1, 2):
         for pair in range(COLOURS):
@@ -200,10 +246,7 @@
         acc, _, total = merged(box3[pair])
         partial += dot((acc / total).astype(BF16), wo[pair * 128 : (pair + 1) * 128, :])
     mine[...] = partial
-    swap = pltpu.make_async_remote_copy(
-        src_ref=mine, dst_ref=theirs, send_sem=pair_send.at[4], recv_sem=pair_recv.at[4],
-        device_id=partner, device_id_type=MESH,
-    )
+    swap = to_partner(2, mine, theirs)
     swap.start()
     swap.wait()
     before = hidden[pl.ds(pl.multiple_of(cell * each, each), each), :].astype(F32) + (mine[...] + theirs[...])
@@ -262,6 +305,20 @@
     for colour in range(COLOURS):
         for digit in range(RING):
             forward(colour, 1 - core, digit).wait_recv()
+    latent = jnp.concatenate([latents[i].reshape(rows, 128) for i in range(2 * COLOURS)], axis=1)
+    shares = []
+    for i, (own, weight, target) in enumerate(((k_own, dk, k_other), (v_own, dv, v_other))):
+        projected = dot(latent, weight[...]).astype(BF16)
+        for pair in range(COLOURS):
+            own[pair] = projected[:, pair * 128 : (pair + 1) * 128]
+        shares.append(to_partner(3 + i, own, target))
+        shares[-1].start()
+
+    @pl.loop(0, COLOURS)
+    def _(pair):
+        scales = [soft[1, first_head + 2 * pair + part] * HD**-0.5 for part in range(2)]
+        att[pair] = attend(q_own[pair], k_own[pair], v_own[pair], scales)
+
     for colour in range(COLOURS):
         for digit in range(RING):
             forward(colour, core, digit).wait_send()
@@ -269,97 +326,103 @@
             for step in range(1, RING):
                 reduce_copy(stage, colour, turn(REDUCE_AXES[colour][stage], step)).wait_send()
                 gather_copy(stage, colour, turn(GATHER_AXES[colour][stage], step)).wait_send()
-    for copy in weights:
+    for copy in shares:
         copy.wait()
 
 
-def decoder(lat, emb, tally, soft, q0, q1, k0, k1, v0, v1, o0, o1, latent_out, tokens, k_scr, v_scr, q_scr, a_scr):
+def decoder(
+    lat, att, q, k, v, o_other, emb_h, tally, soft_h, o_own_h,
+    latent_out, tokens, emb, soft, o_own, wide, other, sem,
+):
     core = lax.axis_index("qgrp")
     blocks, rows, _ = lat.shape
-    group = q0.shape[1]
-    slots = tokens.shape[0]
-    pairs = group // 128
-    own = pl.ds(pl.multiple_of(core * slots, slots), slots)
-    latent = jnp.concatenate([lat[i] for i in range(blocks)], axis=1)
-    latent_out[...] = latent.astype(F32)
-    low = lanes((1, group)) % 128 < HD
-    for side, (wq, wk, wv) in enumerate(((q0, k0, v0), (q1, k1, v1))):
-        at = slice(side * group, (side + 1) * group)
-        q_scr[:, at] = dot(emb[own, :], wq[...]).astype(BF16)
-        keys = dot(latent, wk[...])
-        k_scr[0, :, at] = jnp.where(low, keys, 0.0).astype(BF16)
-        k_scr[1, :, at] = jnp.where(low, 0.0, keys).astype(BF16)
-        values = dot(latent, wv[...]).astype(BF16)
-        for pair in range(pairs):
-            v_scr[side * pairs + pair, :, :128] = values[:, pair * 128 : (pair + 1) * 128]
-            v_scr[side * pairs + pair, :, 128:] = jnp.ones((rows, 128), BF16)
-
-    @pl.loop(0, 2 * pairs)
+    slots, pairs = q.shape[1], q.shape[0]
+    loads = [
+        pltpu.make_async_copy(soft_h, soft, sem.at[0]),
+        pltpu.make_async_copy(emb_h.at[pl.ds(pl.multiple_of(core * slots, slots), slots)], emb, sem.at[1]),
+        pltpu.make_async_copy(o_own_h, o_own, sem.at[2]),
+    ]
+    for copy in loads:
+        copy.start()
+    for i in range(blocks):
+        wide[:, i * 128 : (i + 1) * 128] = lat[i].astype(F32)
+    write = pltpu.make_async_copy(wide, latent_out, sem.at[3])
+    write.start()
+    loads[0].wait()
+    first = (1 - core) * (2 * pairs)
+
+    @pl.loop(0, pairs)
     def _(pair):
-        at = pl.ds(pl.multiple_of(pair * 128, 128), 128)
-        side = lax.rem(core + pair // pairs, 2)
-        first = side * (2 * pairs) + 2 * lax.rem(pair, pairs)
-        halves = []
-        for part in range(2):
-            scale = soft[1, first + part] * HD**-0.5
-            scores = dot_nt(q_scr[:, at], k_scr[part, :, at])
-            top = jnp.max(scores, axis=-1, keepdims=True)
-            weights = jnp.exp2((scores - top) * (scale * LOG2E)).astype(BF16)
-            mixed = dot(weights, v_scr[pair])
-            halves.append(mixed[:, :128] / mixed[:, 128:])
-        a_scr[:, at] = jnp.where(lanes((slots, 128)) < HD, halves[0], halves[1]).astype(BF16)
-
-    update = dot(a_scr[:, :group], o0[...]) + dot(a_scr[:, group:], o1[...])
+        scales = [soft[1, first + 2 * pair + part] * HD**-0.5 for part in range(2)]
+        other[pair] = attend(q[pair], k[pair], v[pair], scales)
+
+    for copy in loads[1:]:
+        copy.wait()
+    own_att = jnp.concatenate([att[i] for i in range(pairs)], axis=1)
+    other_att = jnp.concatenate([other[i] for i in range(pairs)], axis=1)
+    update = dot(own_att, o_own[...]) + dot(other_att, o_other[...])
     position = core * slots + lax.broadcasted_iota(jnp.int32, (slots, 1), 0)
-    tokens[...] = jnp.where(position < tally[0], emb[own, :].astype(F32) + update, 0.0)
+    tokens[...] = jnp.where(position < tally[0], emb[...].astype(F32) + update, 0.0)
+    write.wait()
 
 
 def body(emb, tally, hidden, soft, gq, gk, gv, go, uq, uk, uv, uo, gain):
     rows, group = hidden.shape[0], gq.shape[1]
     slots = emb.shape[0]
+    half = slots // 2
     each = rows // RING**3
     dma = pltpu.SemaphoreType.DMA
-    like = lambda x: jax.ShapeDtypeStruct(x.shape, x.dtype)
+    held = lambda x: pltpu.VMEM(x.shape, x.dtype)
+    emb, hidden, soft, gq, gk, gv, go, uq, uk, uv, uo, gain = (
+        pltpu.with_memory_space_constraint(x, pltpu.HBM)
+        for x in (emb, hidden, soft, gq, gk, gv, go, uq, uk, uv, uo, gain)
+    )
     boxes = []
     for part in (rows // RING, rows // RING**2, each):
         boxes += [pltpu.VMEM((COLOURS, RING, part, 256), BF16)] * 2
-    latents, tq, tk, tv, to = pl.pallas_call(
+    latents, att, q, k, v, o_other = pl.pallas_call(
         gather,
         name="gather",
         out_shape=(
             jax.ShapeDtypeStruct((2 * COLOURS, RING, RING, RING, each, 128), BF16),
-            like(uq), like(uk), like(uv), like(uo),
+            jax.ShapeDtypeStruct((COLOURS, half, 128), BF16),
+            jax.ShapeDtypeStruct((COLOURS, half, 128), BF16),
+            jax.ShapeDtypeStruct((COLOURS, rows, 128), BF16),
+            jax.ShapeDtypeStruct((COLOURS, rows, 128), BF16),
+            jax.ShapeDtypeStruct(uo.shape, BF16),
         ),
-        in_specs=[VMEM, SMEM, VMEM, SMEM, VMEM, VMEM, VMEM, VMEM, VMEM, ANY, ANY, ANY, ANY],
-        out_specs=(VMEM, ANY, ANY, ANY, ANY),
+        in_specs=[HBM, SMEM] + [HBM] * 11,
+        out_specs=(VMEM,) * 6,
         scratch_shapes=[
+            held(emb), held(hidden), pltpu.SMEM(soft.shape, F32), held(gq), held(gk), held(gv), held(go), held(gain),
+            held(uq), held(uk), held(uv), held(uq),
+            pltpu.VMEM((COLOURS, half, 128), BF16),
+            pltpu.VMEM((COLOURS, rows, 128), BF16),
+            pltpu.VMEM((COLOURS, rows, 128), BF16),
             pltpu.VMEM((COLOURS, RING, RING, RING, each, 128), BF16),
             pltpu.VMEM((2, slots, group), BF16),
             pltpu.VMEM((COLOURS, slots, 256), BF16),
             *boxes,
             pltpu.VMEM((each, D), F32),
             pltpu.VMEM((each, D), F32),
-            dma((3, COLOURS, RING)), dma((3, COLOURS, RING)),
+            dma((11,)), dma((3, COLOURS, RING)), dma((3, COLOURS, RING)),
             dma((3, COLOURS, RING)), dma((3, COLOURS, RING)),
             dma((COLOURS, RING)), dma((COLOURS, RING)), dma((5,)), dma((5,)),
         ],
         compiler_params=pltpu.CompilerParams(collective_id=0, has_side_effects=True, vmem_limit_bytes=LIMIT),
     )(emb, tally, hidden, soft, gq, gk, gv, go, gain, uq, uk, uv, uo)
-    half = slots // 2
     return pl.pallas_call(
         decoder,
         name="decoder",
         out_shape=(jax.ShapeDtypeStruct((rows, D), F32), jax.ShapeDtypeStruct((half, D), F32)),
-        in_specs=[VMEM, VMEM, SMEM, SMEM] + [VMEM] * 8,
-        out_specs=(VMEM, VMEM),
+        in_specs=[VMEM] * 6 + [HBM, SMEM, HBM, HBM],
+        out_specs=(HBM, VMEM),
         scratch_shapes=[
-            pltpu.VMEM((2, rows, D), BF16),
-            pltpu.VMEM((2 * COLOURS, rows, 256), BF16),
-            pltpu.VMEM((half, D), BF16),
-            pltpu.VMEM((half, D), BF16),
+            pltpu.VMEM((half, D), BF16), pltpu.SMEM(soft.shape, F32), held(uo), pltpu.VMEM((rows, D), F32),
+            pltpu.VMEM((COLOURS, half, 128), BF16), dma((4,)),
         ],
         compiler_params=pltpu.CompilerParams(vmem_limit_bytes=LIMIT),
-    )(latents.reshape(2 * COLOURS, rows, 128), emb, tally, soft, uq, tq, uk, tk, uv, tv, uo, to)
+    )(latents.reshape(2 * COLOURS, rows, 128), att, q, k, v, o_other, emb, tally, soft, uo)
 
 
 def solution(mesh):

time: 65.2 us -> 57.7 us (0.88)
  Pallas kernels: 63.7 us -> 56.3 us
    pallas_call x1, Pallas kernels: 15.9 us -> 5.27 us  [body(): pl.pallas_call(decoder, name='decoder', out_shape=(jax.ShapeDtypeStruct((...]
    pallas_call x1, Pallas kernels: 47.9 us -> 51 us  [body(): pl.pallas_call(gather, name='gather', out_shape=(jax.ShapeDtypeStruct((2...]
where the time goes in v3:
time: 57.7 us; the launch traced here: 57.6 us
  Pallas kernels  56.3 us (98%)
  between operations  1.29 us (2%)
    pallas_call x1, Pallas kernels, body(): pl.pallas_call(gather, name='gather', out_shape=(jax.ShapeDtypeStruct((2...  51 us
    pallas_call x1, Pallas kernels, body(): pl.pallas_call(decoder, name='decoder', out_shape=(jax.ShapeDtypeStruct((...  5.27 us

profile of v3, /device:TPU:1, one launch (start us, length us, event | category | flops | bytes accessed | tf_op | source)
XLA Modules:
  0.0 57.6 jit_solution(3539143717392055665)
XLA Ops:
  1.3 51.0 %gather.1 = (bf16[6,4,4,4,16,128]{5,4,3,2,1,0:T(8,128)(2,1)S(1)}, bf16[3,256,128]{2,1,0:T(8,128)(2,1)S(1)}, bf16[3,256,128]{2,1,0:T(8,128)(2,1)S(1)}, bf16[3,102...) custom-call(bf16[512,768]{1,0:T(8,128)(2,1)} %emb_h.3, s32[1]{0:T(128)S(6)} %copy.15.tally, ...), custom_call_target="tpu_custom_call" | custom-call | tf_op jit(solution)/shard_map/gather/pallas_call | solution.py:383
  52.3 5.3 %decoder.1 = (f32[1024,768]{1,0:T(8,128)}, f32[256,768]{1,0:T(8,128)}) custom-call(bf16[6,1024,128]{2,1,0:T(8,128)(2,1)S(1)} %bitcast.1, bf16[3,256,128]{2,1,0:T(8,128)(2,1)S(1)} %get-tuple-element.9.att, bf16[3,256,128]{2,1,0:T(8,128)(2,1)S(1)} %get-tuple-element.10.q, bf16[3,1024,128]{2,1,0:T(8,128)(2,1)S(1)} %get-tuple-element.11.k, ...), custom_call_target="tpu_custom_call" | custom-call | tf_op jit(solution)/shard_map/decoder/pallas_call | solution.py:414

commit v4 on v3

--- a/solution.py
+++ b/solution.py
@@ -46,28 +46,23 @@
     return high, middle, rest - middle
 
 
-def packed_stats(top, total):
-    place = lanes(top.shape) % HD
-    packed = jnp.zeros_like(top)
-    for i, part in enumerate(three(top) + three(total)):
-        packed = jnp.where(place == i, part, packed)
-    return packed.astype(BF16)
-
-
-def unpacking():
-    source = lax.broadcasted_iota(jnp.int32, (128, 256), 0)
-    target = lanes((128, 256))
-    same = (target % 128) // HD == source // HD
-    return (same & ((source % HD) // 3 == target // 128)).astype(BF16)
-
-
-def merged(box):
-    count, rows, _ = box.shape
-    stats = dot(box[:, :, 128:].reshape(count * rows, 128), unpacking()).reshape(count, rows, 256)
-    top, total = stats[:, :, :128], stats[:, :, 128:]
-    best = jnp.max(top, axis=0)
-    factor = jnp.exp(top - best)
-    return jnp.sum(factor * box[:, :, :128].astype(F32), axis=0), best, jnp.sum(factor * total, axis=0)
+def columns(rows):
+    width = rows.shape[1]
+    held = jnp.concatenate([rows, jnp.zeros((14, width), F32)], axis=0).astype(BF16)
+    head = lax.broadcasted_iota(jnp.int32, (16, 128), 0)
+    spread = (lanes((16, 128)) // HD == head).astype(BF16)
+    return lax.dot_general(held, spread, (((0,), (0,)), ((), ())), preferred_element_type=F32)
+
+
+def merged(accs, stats):
+    rows = accs.shape[1]
+    best = functools.reduce(jnp.maximum, [stats[i, 0:2] for i in range(RING)])
+    acc, total = 0.0, 0.0
+    for i in range(RING):
+        factor = jnp.exp2(stats[i, 0:2] - best).astype(BF16).astype(F32)
+        total += factor * stats[i, 2:4]
+        acc += columns(factor)[:rows] * accs[i].astype(F32)
+    return acc, best, total
 
 
 def attend(q, k, v, scales):
@@ -92,9 +87,11 @@
     emb_h, tally, hidden_h, soft_h, wq_h, wk_h, wv_h, wo_h, gain_h, dq_h, dk_h, dv_h, do_h,
     latents, att, q_other, k_other, v_other, o_other,
     emb, hidden, soft, wq, wk, wv, wo, gain, dq, dk, dv, dq_other, q_own, k_own, v_own,
-    q_scr, k_scr, v_scr, out1, box1, out2, box2, out3, box3, mine, theirs,
-    load_sem, red_send, red_recv, gat_send, gat_recv, fwd_send, fwd_recv, pair_send, pair_recv,
+    q_scr, k_scr, v_scr, *rest,
 ):
+    outs = (rest[0:2], rest[4:6], rest[8:10])
+    boxes = (rest[2:4], rest[6:8], rest[10:12])
+    mine, theirs, load_sem, red_send, red_recv, gat_send, gat_recv, fwd_send, fwd_recv, pair_send, pair_recv = rest[12:]
     cell, core = lax.axis_index("cell"), lax.axis_index("qgrp")
     here = (cell // 16, (cell // 4) % 4, cell % 4)
     partner = (cell, 1 - core)
@@ -133,23 +130,32 @@
             pl.semaphore_signal(barrier, inc=1, device_id=peer(axis, turn(axis, step)), device_id_type=MESH)
     pl.semaphore_signal(barrier, inc=1, device_id=partner, device_id_type=MESH)
 
-    ready("emb", "wk")
-    keys = dot(emb[...], wk[...])
-    low = lanes((1, group)) % 128 < HD
-    k_scr[0] = jnp.where(low, keys, 0.0).astype(BF16)
-    k_scr[1] = jnp.where(low, 0.0, keys).astype(BF16)
+    first_head = core * (2 * COLOURS)
+    first = lanes((1, 128)) < HD
+    valid = lax.broadcasted_iota(jnp.int32, (slots, 1), 0) < tally[0]
+    ready("emb", "wk", "soft")
+    keys = dot(emb[...], wk[...]).astype(BF16).astype(F32)
+    keys = jnp.where(valid, keys, keys[0:1])
+    for pair in range(COLOURS):
+        scale = [soft[0, first_head + 2 * pair + part] * (HD**-0.5 * LOG2E) for part in range(2)]
+        scaled = keys[:, pair * 128 : (pair + 1) * 128] * jnp.where(first, scale[0], scale[1])
+        high = scaled.astype(BF16).astype(F32)
+        rest = scaled - high
+        k_scr[2 * pair] = jnp.where(first, high, pltpu.roll(rest, HD, 1)).astype(BF16)
+        k_scr[2 * pair + 1] = jnp.where(first, pltpu.roll(high, HD, 1), rest).astype(BF16)
     ready("wv")
-    values = dot(emb[...], wv[...]).astype(BF16)
+    values = jnp.where(valid, dot(emb[...], wv[...]), 0.0).astype(BF16)
     for pair in range(COLOURS):
         v_scr[pair, :, :128] = values[:, pair * 128 : (pair + 1) * 128]
-        v_scr[pair, :, 128:] = jnp.ones((slots, 128), BF16)
+        v_scr[pair, :, 128:] = jnp.broadcast_to(jnp.where(valid, 1.0, 0.0), (slots, 128)).astype(BF16)
     ready("hidden", "wq")
-    queries = dot(hidden[...], wq[...]).astype(BF16)
-    for pair in range(COLOURS):
-        q_scr[pair] = queries[:, pair * 128 : (pair + 1) * 128].reshape(RING, RING, RING, each, 128)
-    bias = jnp.where(lanes((1, slots)) < tally[0], 0.0, MASKED)
-    first_head = core * (2 * COLOURS)
-    ready("soft")
+    queries = dot(hidden[...], wq[...])
+    for pair in range(COLOURS):
+        one = queries[:, pair * 128 : (pair + 1) * 128]
+        other = pltpu.roll(one, HD, 1)
+        for part in range(2):
+            double = jnp.where(first == (part == 0), one, other).astype(BF16)
+            q_scr[2 * pair + part] = double.reshape(RING, RING, RING, each, 128)
 
     pl.semaphore_wait(barrier, 10)
     swaps = [to_partner(0, dq_h, dq_other), to_partner(1, do_h, o_other)]
@@ -157,54 +163,55 @@
         copy.start()
 
     def tile(pair, digit):
-        axis = REDUCE_AXES[pair][0]
-        q = q_scr[(pair,) + tuple(digit if i == axis else slice(None) for i in range(axis + 1))]
-        q = q.reshape(quarter, 128)
-        first = lanes((quarter, 128)) < HD
-        tops, halves = [], []
+        axis, following, _ = REDUCE_AXES[pair]
+        rest = [i for i in range(3) if i != axis]
+        where = tuple(digit if i == axis else slice(None) for i in range(axis + 1))
+        tops, both = [], []
         for part in range(2):
-            scale = soft[0, first_head + 2 * pair + part] * HD**-0.5
-            scores = dot_nt(q, k_scr[part, :, pair * 128 : (pair + 1) * 128]) + bias
-            top = jnp.max(scores, axis=-1, keepdims=True)
-            weight = jnp.exp2((scores - top) * (scale * LOG2E)).astype(BF16)
-            halves.append(dot(weight, v_scr[pair]))
-            tops.append(top * scale)
-        mixed = jnp.where(first, halves[0][:, :128], halves[1][:, :128])
-        total = jnp.where(first, halves[0][:, 128:], halves[1][:, 128:])
-        return mixed.astype(BF16), packed_stats(jnp.where(first, tops[0], tops[1]), total)
-
-    outs, boxes = (out1, out2, out3), (box1, box2, box3)
+            q = q_scr[(2 * pair + part,) + where]
+            if rest[0] != following:
+                q = jnp.concatenate([q[:, i].reshape(RING * each, 128) for i in range(RING)], axis=0)
+            scores = dot_nt(q.reshape(quarter, 128), k_scr[2 * pair + part])
+            tops.append(jnp.max(scores, axis=-1, keepdims=True))
+            both.append(dot(jnp.exp2(scores - tops[-1]).astype(BF16), v_scr[pair]))
+        acc = jnp.where(first, both[0][:, :128], both[1][:, :128]).astype(BF16)
+        lane = lanes((1, 128))
+        stats = jnp.where(lane == 0, tops[0], jnp.where(lane == 1, tops[1], jnp.where(lane == 2, both[0][:, 128:], both[1][:, 128:])))
+        return acc, stats.T[0:8]
 
     def reduce_copy(stage, pair, digit):
         axis = REDUCE_AXES[pair][stage]
-        return pltpu.make_async_remote_copy(
-            src_ref=outs[stage].at[pair, digit], dst_ref=boxes[stage].at[pair, here[axis]],
-            send_sem=red_send.at[stage, pair, digit], recv_sem=red_recv.at[stage, pair, here[axis]],
-            device_id=peer(axis, digit), device_id_type=MESH,
-        )
+        return [
+            pltpu.make_async_remote_copy(
+                src_ref=outs[stage][i].at[pair, digit], dst_ref=boxes[stage][i].at[pair, here[axis]],
+                send_sem=red_send.at[stage, pair, digit, i], recv_sem=red_recv.at[stage, pair, here[axis], i],
+                device_id=peer(axis, digit), device_id_type=MESH,
+            )
+            for i in range(2)
+        ]
 
     def reduce_arrived(stage, pair, digit):
         axis = REDUCE_AXES[pair][stage]
-        pltpu.make_async_remote_copy(
-            src_ref=outs[stage].at[pair, digit], dst_ref=boxes[stage].at[pair, digit],
-            send_sem=red_send.at[stage, pair, digit], recv_sem=red_recv.at[stage, pair, digit],
-            device_id=peer(axis, digit), device_id_type=MESH,
-        ).wait_recv()
-
-    @pl.loop(1, RING)
-    def _(step):
-        for pair in range(COLOURS):
-            digit = turn(REDUCE_AXES[pair][0], step)
-            mixed, stats = tile(pair, digit)
-            out1[pair, digit, :, :128] = mixed
-            out1[pair, digit, :, 128:] = stats
-            reduce_copy(0, pair, digit).start()
+        for i in range(2):
+            pltpu.make_async_remote_copy(
+                src_ref=outs[stage][i].at[pair, digit], dst_ref=boxes[stage][i].at[pair, digit],
+                send_sem=red_send.at[stage, pair, digit, i], recv_sem=red_recv.at[stage, pair, digit, i],
+                device_id=peer(axis, digit), device_id_type=MESH,
+            ).wait_recv()
+
+    @pl.loop(0, RING - 1)
+    def _(i):
+        step = lax.rem(2 + i + i * (i - 1) // 2, RING)
+        digits = [turn(REDUCE_AXES[pair][0], step) for pair in range(COLOURS)]
+        for pair in range(COLOURS):
+            outs[0][0][pair, digits[pair]], outs[0][1][pair, digits[pair]] = tile(pair, digits[pair])
+        for pair in range(COLOURS):
+            for copy in reduce_copy(0, pair, digits[pair]):
+                copy.start()
 
     for pair in range(COLOURS):
         own = here[REDUCE_AXES[pair][0]]
-        mixed, stats = tile(pair, own)
-        box1[pair, own, :, :128] = mixed
-        box1[pair, own, :, 128:] = stats
+        boxes[0][0][pair, own], boxes[0][1][pair, own] = tile(pair, own)
 
     half = slots // 2
     ready("dq", "wo", "gain", "dk", "dv")
@@ -221,30 +228,33 @@
         for pair in range(COLOURS):
             for step in range(1, RING):
                 reduce_arrived(stage - 1, pair, turn(REDUCE_AXES[pair][stage - 1], step))
-            acc, top, total = merged(boxes[stage - 1][pair])
-            joined = jnp.concatenate([acc.astype(BF16), packed_stats(top, total)], axis=1)
+        part = rows // RING ** (stage + 1)
+        for pair in range(COLOURS):
+            acc, top, total = merged(*(box.at[pair] for box in boxes[stage - 1]))
+            stats = jnp.concatenate([top, total, jnp.zeros((4, top.shape[1]), F32)], axis=0)
+            for i in range(RING):
+                outs[stage][0][pair, i] = acc[i * part : (i + 1) * part].astype(BF16)
+                outs[stage][1][pair, i] = jnp.concatenate(
+                    [stats[:, i * part : (i + 1) * part], jnp.zeros((8, 128 - part), F32)], axis=1
+                )
+        for pair in range(COLOURS):
             axis = REDUCE_AXES[pair][stage]
-            if stage == 1:
-                joined = joined.reshape(RING, RING, each, 256)
-                rest = [i for i in range(3) if i != REDUCE_AXES[pair][0]]
-                pieces = [
-                    (joined[i] if rest[0] == axis else joined[:, i]).reshape(RING * each, 256)
-                    for i in range(RING)
-                ]
-            else:
-                pieces = [joined[i * each : (i + 1) * each] for i in range(RING)]
-            for i in range(RING):
-                outs[stage][pair, i] = pieces[i]
-            boxes[stage][pair, here[axis]] = outs[stage][pair, here[axis]]
-            for step in range(1, RING):
-                reduce_copy(stage, pair, turn(axis, step)).start()
-
-    partial = jnp.zeros((each, D), F32)
+            for step in (2, 1, 3):
+                for copy in reduce_copy(stage, pair, turn(axis, step)):
+                    copy.start()
+        for pair in range(COLOURS):
+            own = here[REDUCE_AXES[pair][stage]]
+            for i in range(2):
+                boxes[stage][i][pair, own] = outs[stage][i][pair, own]
+
     for pair in range(COLOURS):
         for step in range(1, RING):
             reduce_arrived(2, pair, turn(REDUCE_AXES[pair][2], step))
-        acc, _, total = merged(box3[pair])
-        partial += dot((acc / total).astype(BF16), wo[pair * 128 : (pair + 1) * 128, :])
+    partial = jnp.zeros((each, D), F32)
+    for pair in range(COLOURS):
+        acc, _, total = merged(*(box.at[pair] for box in boxes[2]))
+        inverse = sum(columns(x)[:each] for x in three(1.0 / jnp.where(lanes(total.shape) < each, total, 1.0)))
+        partial += dot((acc * inverse).astype(BF16), wo[pair * 128 : (pair + 1) * 128, :])
     mine[...] = partial
     swap = to_partner(2, mine, theirs)
     swap.start()
@@ -314,8 +324,7 @@
         shares.append(to_partner(3 + i, own, target))
         shares[-1].start()
 
-    @pl.loop(0, COLOURS)
-    def _(pair):
+    for pair in range(COLOURS):
         scales = [soft[1, first_head + 2 * pair + part] * HD**-0.5 for part in range(2)]
         att[pair] = attend(q_own[pair], k_own[pair], v_own[pair], scales)
 
@@ -324,7 +333,8 @@
             forward(colour, core, digit).wait_send()
         for stage in range(3):
             for step in range(1, RING):
-                reduce_copy(stage, colour, turn(REDUCE_AXES[colour][stage], step)).wait_send()
+                for copy in reduce_copy(stage, colour, turn(REDUCE_AXES[colour][stage], step)):
+                    copy.wait_send()
                 gather_copy(stage, colour, turn(GATHER_AXES[colour][stage], step)).wait_send()
     for copy in shares:
         copy.wait()
@@ -351,8 +361,7 @@
     loads[0].wait()
     first = (1 - core) * (2 * pairs)
 
-    @pl.loop(0, pairs)
-    def _(pair):
+    for pair in range(pairs):
         scales = [soft[1, first + 2 * pair + part] * HD**-0.5 for part in range(2)]
         other[pair] = attend(q[pair], k[pair], v[pair], scales)
 
@@ -379,7 +388,10 @@
     )
     boxes = []
     for part in (rows // RING, rows // RING**2, each):
-        boxes += [pltpu.VMEM((COLOURS, RING, part, 256), BF16)] * 2
+        boxes += [
+            pltpu.VMEM((COLOURS, RING, part, 128), BF16),
+            pltpu.VMEM((COLOURS, RING, 8, max(part, 128)), F32),
+        ] * 2
     latents, att, q, k, v, o_other = pl.pallas_call(
         gather,
         name="gather",
@@ -399,13 +411,13 @@
             pltpu.VMEM((COLOURS, half, 128), BF16),
             pltpu.VMEM((COLOURS, rows, 128), BF16),
             pltpu.VMEM((COLOURS, rows, 128), BF16),
-            pltpu.VMEM((COLOURS, RING, RING, RING, each, 128), BF16),
-            pltpu.VMEM((2, slots, group), BF16),
+            pltpu.VMEM((2 * COLOURS, RING, RING, RING, each, 128), BF16),
+            pltpu.VMEM((2 * COLOURS, slots, 128), BF16),
             pltpu.VMEM((COLOURS, slots, 256), BF16),
             *boxes,
             pltpu.VMEM((each, D), F32),
             pltpu.VMEM((each, D), F32),
-            dma((11,)), dma((3, COLOURS, RING)), dma((3, COLOURS, RING)),
+            dma((11,)), dma((3, COLOURS, RING, 2)), dma((3, COLOURS, RING, 2)),
             dma((3, COLOURS, RING)), dma((3, COLOURS, RING)),
             dma((COLOURS, RING)), dma((COLOURS, RING)), dma((5,)), dma((5,)),
         ],

time: 57.7 us -> 52.8 us (0.915)
  Pallas kernels: 56.3 us -> 51.4 us
    pallas_call x1, Pallas kernels: 51 us -> 47 us  [body(): pl.pallas_call(gather, name='gather', out_shape=(jax.ShapeDtypeStruct((2...]
    pallas_call x1, Pallas kernels: 5.27 us -> 4.4 us  [body(): pl.pallas_call(decoder, name='decoder', out_shape=(jax.ShapeDtypeStruct((...]
where the time goes in v4:
time: 52.8 us; the launch traced here: 52.7 us
  Pallas kernels  51.4 us (97%)
  between operations  1.29 us (2%)
    pallas_call x1, Pallas kernels, body(): pl.pallas_call(gather, name='gather', out_shape=(jax.ShapeDtypeStruct((2...  47 us
    pallas_call x1, Pallas kernels, body(): pl.pallas_call(decoder, name='decoder', out_shape=(jax.ShapeDtypeStruct((...  4.4 us

profile of v4, /device:TPU:1, one launch (start us, length us, event | category | flops | bytes accessed | tf_op | source)
XLA Modules:
  0.0 52.7 jit_solution(11994258279948831831)
XLA Ops:
  1.3 47.0 %gather.1 = (bf16[6,4,4,4,16,128]{5,4,3,2,1,0:T(8,128)(2,1)S(1)}, bf16[3,256,128]{2,1,0:T(8,128)(2,1)S(1)}, bf16[3,256,128]{2,1,0:T(8,128)(2,1)S(1)}, bf16[3,102...) custom-call(bf16[512,768]{1,0:T(8,128)(2,1)} %emb_h.3, s32[1]{0:T(128)S(6)} %copy.15.tally, ...), custom_call_target="tpu_custom_call" | custom-call | tf_op jit(solution)/shard_map/gather/pallas_call | solution.py:395
  48.3 4.4 %decoder.1 = (f32[1024,768]{1,0:T(8,128)}, f32[256,768]{1,0:T(8,128)}) custom-call(bf16[6,1024,128]{2,1,0:T(8,128)(2,1)S(1)} %bitcast.1, bf16[3,256,128]{2,1,0:T(8,128)(2,1)S(1)} %get-tuple-element.9.att, bf16[3,256,128]{2,1,0:T(8,128)(2,1)S(1)} %get-tuple-element.10.q, bf16[3,1024,128]{2,1,0:T(8,128)(2,1)S(1)} %get-tuple-element.11.k, ...), custom_call_target="tpu_custom_call" | custom-call | tf_op jit(solution)/shard_map/decoder/pallas_call | solution.py:426

commit v5 on v4

--- a/solution.py
+++ b/solution.py
@@ -85,13 +85,13 @@
 
 def gather(
     emb_h, tally, hidden_h, soft_h, wq_h, wk_h, wv_h, wo_h, gain_h, dq_h, dk_h, dv_h, do_h,
-    latents, att, q_other, k_other, v_other, o_other,
-    emb, hidden, soft, wq, wk, wv, wo, gain, dq, dk, dv, dq_other, q_own, k_own, v_own,
+    latents, att, att_other, o_other,
+    emb, hidden, soft, wq, wk, wv, wo, gain, dq, dk, dv, q_own, k_own, v_own, att_send,
     q_scr, k_scr, v_scr, *rest,
 ):
     outs = (rest[0:2], rest[4:6], rest[8:10])
     boxes = (rest[2:4], rest[6:8], rest[10:12])
-    mine, theirs, load_sem, red_send, red_recv, gat_send, gat_recv, fwd_send, fwd_recv, pair_send, pair_recv = rest[12:]
+    mine, theirs, load_sem, red_send, red_recv, gat_send, gat_recv, last_recv, fwd_send, fwd_recv, pair_send, pair_recv = rest[12:]
     cell, core = lax.axis_index("cell"), lax.axis_index("qgrp")
     here = (cell // 16, (cell // 4) % 4, cell % 4)
     partner = (cell, 1 - core)
@@ -133,7 +133,7 @@
     first_head = core * (2 * COLOURS)
     first = lanes((1, 128)) < HD
     valid = lax.broadcasted_iota(jnp.int32, (slots, 1), 0) < tally[0]
-    ready("emb", "wk", "soft")
+    ready("emb", "wk", "soft", "wv")
     keys = dot(emb[...], wk[...]).astype(BF16).astype(F32)
     keys = jnp.where(valid, keys, keys[0:1])
     for pair in range(COLOURS):
@@ -143,7 +143,6 @@
         rest = scaled - high
         k_scr[2 * pair] = jnp.where(first, high, pltpu.roll(rest, HD, 1)).astype(BF16)
         k_scr[2 * pair + 1] = jnp.where(first, pltpu.roll(high, HD, 1), rest).astype(BF16)
-    ready("wv")
     values = jnp.where(valid, dot(emb[...], wv[...]), 0.0).astype(BF16)
     for pair in range(COLOURS):
         v_scr[pair, :, :128] = values[:, pair * 128 : (pair + 1) * 128]
@@ -158,9 +157,8 @@
             q_scr[2 * pair + part] = double.reshape(RING, RING, RING, each, 128)
 
     pl.semaphore_wait(barrier, 10)
-    swaps = [to_partner(0, dq_h, dq_other), to_partner(1, do_h, o_other)]
-    for copy in swaps:
-        copy.start()
+    trade = to_partner(0, do_h, o_other)
+    trade.start()
 
     def tile(pair, digit):
         axis, following, _ = REDUCE_AXES[pair]
@@ -184,20 +182,21 @@
         return [
             pltpu.make_async_remote_copy(
                 src_ref=outs[stage][i].at[pair, digit], dst_ref=boxes[stage][i].at[pair, here[axis]],
-                send_sem=red_send.at[stage, pair, digit, i], recv_sem=red_recv.at[stage, pair, here[axis], i],
+                send_sem=red_send.at[stage, i], recv_sem=red_recv.at[stage, i],
                 device_id=peer(axis, digit), device_id_type=MESH,
             )
             for i in range(2)
         ]
 
-    def reduce_arrived(stage, pair, digit):
-        axis = REDUCE_AXES[pair][stage]
-        for i in range(2):
+    def reduce_all(stage):
+        return [
             pltpu.make_async_remote_copy(
-                src_ref=outs[stage][i].at[pair, digit], dst_ref=boxes[stage][i].at[pair, digit],
-                send_sem=red_send.at[stage, pair, digit, i], recv_sem=red_recv.at[stage, pair, digit, i],
-                device_id=peer(axis, digit), device_id_type=MESH,
-            ).wait_recv()
+                src_ref=outs[stage][i].at[:, pl.ds(0, RING - 1)], dst_ref=boxes[stage][i].at[:, pl.ds(0, RING - 1)],
+                send_sem=red_send.at[stage, i], recv_sem=red_recv.at[stage, i],
+                device_id=partner, device_id_type=MESH,
+            )
+            for i in range(2)
+        ]
 
     @pl.loop(0, RING - 1)
     def _(i):
@@ -215,19 +214,13 @@
 
     half = slots // 2
     ready("dq", "wo", "gain", "dk", "dv")
-    mine_rows = emb[pl.ds(pl.multiple_of(core * half, half), half), :]
-    for target, weight in ((q_own, dq), (q_other, dq_other)):
-        if weight is dq_other:
-            for copy in swaps:
-                copy.wait()
-        projected = dot(mine_rows, weight[...]).astype(BF16)
-        for pair in range(COLOURS):
-            target[pair] = projected[:, pair * 128 : (pair + 1) * 128]
+    projected = dot(emb[...], dq[...]).astype(BF16)
+    for pair in range(COLOURS):
+        q_own[pair] = projected[:, pair * 128 : (pair + 1) * 128]
 
     for stage in (1, 2):
-        for pair in range(COLOURS):
-            for step in range(1, RING):
-                reduce_arrived(stage - 1, pair, turn(REDUCE_AXES[pair][stage - 1], step))
+        for copy in reduce_all(stage - 1):
+            copy.wait_recv()
         part = rows // RING ** (stage + 1)
         for pair in range(COLOURS):
             acc, top, total = merged(*(box.at[pair] for box in boxes[stage - 1]))
@@ -247,9 +240,8 @@
             for i in range(2):
                 boxes[stage][i][pair, own] = outs[stage][i][pair, own]
 
-    for pair in range(COLOURS):
-        for step in range(1, RING):
-            reduce_arrived(2, pair, turn(REDUCE_AXES[pair][2], step))
+    for copy in reduce_all(2):
+        copy.wait_recv()
     partial = jnp.zeros((each, D), F32)
     for pair in range(COLOURS):
         acc, _, total = merged(*(box.at[pair] for box in boxes[2]))
@@ -275,101 +267,105 @@
 
     def gather_copy(stage, colour, digit):
         axis = GATHER_AXES[colour][stage]
+        arrival = last_recv.at[colour, here[axis]] if stage == 2 else gat_recv.at[stage, colour]
         return pltpu.make_async_remote_copy(
             src_ref=slab(colour, core, stage), dst_ref=slab(colour, core, stage),
-            send_sem=gat_send.at[stage, colour, digit], recv_sem=gat_recv.at[stage, colour, here[axis]],
+            send_sem=gat_send.at[stage, colour], recv_sem=arrival,
             device_id=peer(axis, digit), device_id_type=MESH,
         )
 
-    def gather_arrived(stage, colour, digit):
-        axis = GATHER_AXES[colour][stage]
-        pltpu.make_async_remote_copy(
-            src_ref=slab(colour, core, stage), dst_ref=slab(colour, core, stage, axis, digit),
-            send_sem=gat_send.at[stage, colour, digit], recv_sem=gat_recv.at[stage, colour, digit],
+    def gather_all(stage, colour):
+        part = latents.at[(2 * colour + core,) + (0,) * (2 - stage) + (pl.ds(0, RING - 1),)]
+        return pltpu.make_async_remote_copy(
+            src_ref=part, dst_ref=part, send_sem=gat_send.at[stage, colour],
+            recv_sem=gat_recv.at[min(stage, 1), colour], device_id=partner, device_id_type=MESH,
+        )
+
+    def gather_last(colour, digit):
+        axis = GATHER_AXES[colour][2]
+        return pltpu.make_async_remote_copy(
+            src_ref=slab(colour, core, 2), dst_ref=slab(colour, core, 2, axis, digit),
+            send_sem=gat_send.at[2, colour], recv_sem=last_recv.at[colour, digit],
             device_id=peer(axis, digit), device_id_type=MESH,
-        ).wait_recv()
-
-    def forward(colour, side, digit):
-        axis = GATHER_AXES[colour][2]
-        part = slab(colour, side, 2, axis, digit)
+        )
+
+    def forward(colour, part):
         return pltpu.make_async_remote_copy(
-            src_ref=part, dst_ref=part, send_sem=fwd_send.at[colour, digit], recv_sem=fwd_recv.at[colour, digit],
+            src_ref=part, dst_ref=part, send_sem=fwd_send.at[colour], recv_sem=fwd_recv.at[colour],
             device_id=partner, device_id_type=MESH,
         )
 
     for stage in range(3):
         for colour in range(COLOURS):
             if stage:
-                for step in range(1, RING):
-                    gather_arrived(stage - 1, colour, turn(GATHER_AXES[colour][stage - 1], step))
+                gather_all(stage - 1, colour).wait_recv()
             axis = GATHER_AXES[colour][stage]
-            for step in range(1, RING):
+            for step in (2, 1, 3):
                 gather_copy(stage, colour, turn(axis, step)).start()
             if stage == 2:
-                forward(colour, core, here[axis]).start()
+                forward(colour, slab(colour, core, 2)).start()
+        for copy in reduce_all(stage):
+            copy.wait_send()
     for step in (1, 3, 2):
         for colour in range(COLOURS):
-            digit = turn(GATHER_AXES[colour][2], step)
-            gather_arrived(2, colour, digit)
-            forward(colour, core, digit).start()
+            axis = GATHER_AXES[colour][2]
+            digit = turn(axis, step)
+            gather_last(colour, digit).wait_recv()
+            forward(colour, slab(colour, core, 2, axis, digit)).start()
+    for stage in range(2):
+        for colour in range(COLOURS):
+            gather_all(stage, colour).wait_send()
     for colour in range(COLOURS):
-        for digit in range(RING):
-            forward(colour, 1 - core, digit).wait_recv()
+        forward(colour, latents.at[2 * colour + 1 - core]).wait_recv()
     latent = jnp.concatenate([latents[i].reshape(rows, 128) for i in range(2 * COLOURS)], axis=1)
-    shares = []
-    for i, (own, weight, target) in enumerate(((k_own, dk, k_other), (v_own, dv, v_other))):
+    for own, weight in ((k_own, dk), (v_own, dv)):
         projected = dot(latent, weight[...]).astype(BF16)
         for pair in range(COLOURS):
             own[pair] = projected[:, pair * 128 : (pair + 1) * 128]
-        shares.append(to_partner(3 + i, own, target))
-        shares[-1].start()
-
-    for pair in range(COLOURS):
+
+    def attended(pair, side):
+        q = q_own[pair, pl.ds(pl.multiple_of(side * half, half), half)]
         scales = [soft[1, first_head + 2 * pair + part] * HD**-0.5 for part in range(2)]
-        att[pair] = attend(q_own[pair], k_own[pair], v_own[pair], scales)
+        return attend(q, k_own[pair], v_own[pair], scales)
+
+    shares = [to_partner(i, att_send.at[pair], att_other.at[pair]) for pair, i in enumerate((1, 3, 4))]
+    for pair in range(COLOURS):
+        att_send[pair] = attended(pair, 1 - core)
+    for copy in shares:
+        copy.start()
+    for pair in range(COLOURS):
+        att[pair] = attended(pair, core)
 
     for colour in range(COLOURS):
-        for digit in range(RING):
-            forward(colour, core, digit).wait_send()
-        for stage in range(3):
-            for step in range(1, RING):
-                for copy in reduce_copy(stage, colour, turn(REDUCE_AXES[colour][stage], step)):
-                    copy.wait_send()
-                gather_copy(stage, colour, turn(GATHER_AXES[colour][stage], step)).wait_send()
+        forward(colour, latents.at[2 * colour + core]).wait_send()
+        gather_all(2, colour).wait_send()
+    trade.wait()
     for copy in shares:
         copy.wait()
 
 
 def decoder(
-    lat, att, q, k, v, o_other, emb_h, tally, soft_h, o_own_h,
-    latent_out, tokens, emb, soft, o_own, wide, other, sem,
+    lat, att, att_other, o_other, emb_h, tally, o_own_h,
+    latent_out, tokens, emb, o_own, wide, sem,
 ):
     core = lax.axis_index("qgrp")
-    blocks, rows, _ = lat.shape
-    slots, pairs = q.shape[1], q.shape[0]
+    blocks = lat.shape[0]
+    pairs, slots, _ = att.shape
     loads = [
-        pltpu.make_async_copy(soft_h, soft, sem.at[0]),
-        pltpu.make_async_copy(emb_h.at[pl.ds(pl.multiple_of(core * slots, slots), slots)], emb, sem.at[1]),
-        pltpu.make_async_copy(o_own_h, o_own, sem.at[2]),
+        pltpu.make_async_copy(emb_h.at[pl.ds(pl.multiple_of(core * slots, slots), slots)], emb, sem.at[0]),
+        pltpu.make_async_copy(o_own_h, o_own, sem.at[1]),
     ]
     for copy in loads:
         copy.start()
     for i in range(blocks):
         wide[:, i * 128 : (i + 1) * 128] = lat[i].astype(F32)
-    write = pltpu.make_async_copy(wide, latent_out, sem.at[3])
+    write = pltpu.make_async_copy(wide, latent_out, sem.at[2])
     write.start()
-    loads[0].wait()
-    first = (1 - core) * (2 * pairs)
-
-    for pair in range(pairs):
-        scales = [soft[1, first + 2 * pair + part] * HD**-0.5 for part in range(2)]
-        other[pair] = attend(q[pair], k[pair], v[pair], scales)
-
-    for copy in loads[1:]:
+    for copy in loads:
         copy.wait()
-    own_att = jnp.concatenate([att[i] for i in range(pairs)], axis=1)
-    other_att = jnp.concatenate([other[i] for i in range(pairs)], axis=1)
-    update = dot(own_att, o_own[...]) + dot(other_att, o_other[...])
+    own = jnp.concatenate([att[i] for i in range(pairs)], axis=1)
+    other = jnp.concatenate([att_other[i] for i in range(pairs)], axis=1)
+    update = dot(own, o_own[...]) + dot(other, o_other[...])
     position = core * slots + lax.broadcasted_iota(jnp.int32, (slots, 1), 0)
     tokens[...] = jnp.where(position < tally[0], emb[...].astype(F32) + update, 0.0)
     write.wait()
@@ -392,34 +388,32 @@
             pltpu.VMEM((COLOURS, RING, part, 128), BF16),
             pltpu.VMEM((COLOURS, RING, 8, max(part, 128)), F32),
         ] * 2
-    latents, att, q, k, v, o_other = pl.pallas_call(
+    latents, att, att_other, o_other = pl.pallas_call(
         gather,
         name="gather",
         out_shape=(
             jax.ShapeDtypeStruct((2 * COLOURS, RING, RING, RING, each, 128), BF16),
             jax.ShapeDtypeStruct((COLOURS, half, 128), BF16),
             jax.ShapeDtypeStruct((COLOURS, half, 128), BF16),
-            jax.ShapeDtypeStruct((COLOURS, rows, 128), BF16),
-            jax.ShapeDtypeStruct((COLOURS, rows, 128), BF16),
             jax.ShapeDtypeStruct(uo.shape, BF16),
         ),
         in_specs=[HBM, SMEM] + [HBM] * 11,
-        out_specs=(VMEM,) * 6,
+        out_specs=(VMEM,) * 4,
         scratch_shapes=[
             held(emb), held(hidden), pltpu.SMEM(soft.shape, F32), held(gq), held(gk), held(gv), held(go), held(gain),
-            held(uq), held(uk), held(uv), held(uq),
-            pltpu.VMEM((COLOURS, half, 128), BF16),
+            held(uq), held(uk), held(uv),
+            pltpu.VMEM((COLOURS, slots, 128), BF16),
             pltpu.VMEM((COLOURS, rows, 128), BF16),
             pltpu.VMEM((COLOURS, rows, 128), BF16),
+            pltpu.VMEM((COLOURS, half, 128), BF16),
             pltpu.VMEM((2 * COLOURS, RING, RING, RING, each, 128), BF16),
             pltpu.VMEM((2 * COLOURS, slots, 128), BF16),
             pltpu.VMEM((COLOURS, slots, 256), BF16),
             *boxes,
             pltpu.VMEM((each, D), F32),
             pltpu.VMEM((each, D), F32),
-            dma((11,)), dma((3, COLOURS, RING, 2)), dma((3, COLOURS, RING, 2)),
-            dma((3, COLOURS, RING)), dma((3, COLOURS, RING)),
-            dma((COLOURS, RING)), dma((COLOURS, RING)), dma((5,)), dma((5,)),
+            dma((11,)), dma((3, 2)), dma((3, 2)), dma((3, COLOURS)), dma((2, COLOURS)), dma((COLOURS, RING)),
+            dma((COLOURS,)), dma((COLOURS,)), dma((5,)), dma((5,)),
         ],
         compiler_params=pltpu.CompilerParams(collective_id=0, has_side_effects=True, vmem_limit_bytes=LIMIT),
     )(emb, tally, hidden, soft, gq, gk, gv, go, gain, uq, uk, uv, uo)
@@ -427,14 +421,11 @@
         decoder,
         name="decoder",
         out_shape=(jax.ShapeDtypeStruct((rows, D), F32), jax.ShapeDtypeStruct((half, D), F32)),
-        in_specs=[VMEM] * 6 + [HBM, SMEM, HBM, HBM],
+        in_specs=[VMEM] * 4 + [HBM, SMEM, HBM],
         out_specs=(HBM, VMEM),
-        scratch_shapes=[
-            pltpu.VMEM((half, D), BF16), pltpu.SMEM(soft.shape, F32), held(uo), pltpu.VMEM((rows, D), F32),
-            pltpu.VMEM((COLOURS, half, 128), BF16), dma((4,)),
-        ],
+        scratch_shapes=[pltpu.VMEM((half, D), BF16), held(uo), pltpu.VMEM((rows, D), F32), dma((3,))],
         compiler_params=pltpu.CompilerParams(vmem_limit_bytes=LIMIT),
-    )(latents.reshape(2 * COLOURS, rows, 128), att, q, k, v, o_other, emb, tally, soft, uo)
+    )(latents.reshape(2 * COLOURS, rows, 128), att, att_other, o_other, emb, tally, uo)
 
 
 def solution(mesh):

time: 52.8 us -> 51 us (0.966)
  Pallas kernels: 51.4 us -> 49.5 us
    pallas_call x1, Pallas kernels: 4.4 us -> 2.83 us  [body(): pl.pallas_call(decoder, name='decoder', out_shape=(jax.ShapeDtypeStruct((...]
where the time goes in v5:
time: 51 us; the launch traced here: 50.8 us
  Pallas kernels  49.5 us (97%)
  between operations  1.29 us (3%)
    pallas_call x1, Pallas kernels, body(): pl.pallas_call(gather, name='gather', out_shape=(jax.ShapeDtypeStruct((2...  46.7 us
    pallas_call x1, Pallas kernels, body(): pl.pallas_call(decoder, name='decoder', out_shape=(jax.ShapeDtypeStruct((...  2.83 us

profile of v5, /device:TPU:1, one launch (start us, length us, event | category | flops | bytes accessed | tf_op | source)
XLA Modules:
  0.0 50.8 jit_solution(10287504383916546021)
XLA Ops:
  1.3 46.7 %gather.1 = (bf16[6,4,4,4,16,128]{5,4,3,2,1,0:T(8,128)(2,1)S(1)}, bf16[3,256,128]{2,1,0:T(8,128)(2,1)S(1)}, bf16[3,256,128]{2,1,0:T(8,128)(2,1)S(1)}, bf16[384,768]{1,0:T(8,128)(2,1)S(1)}) custom-call(bf16[512,768]{1,0:T(8,128)(2,1)} %emb_h.3, s32[1]{0:T(128)S(6)} %copy.15.tally, bf16[1024,768]{1,0:T(8,128)(2,1)} %hidden_h.1, f32[2,12]{1,0:T(2,128)} %soft_h.1, ...), custom_call_target="tpu_custom_call" | custom-call | tf_op jit(solution)/shard_map/gather/pallas_call | solution.py:391
  48.0 2.8 %decoder.1 = (f32[1024,768]{1,0:T(8,128)}, f32[256,768]{1,0:T(8,128)}) custom-call(bf16[6,1024,128]{2,1,0:T(8,128)(2,1)S(1)} %bitcast.1, bf16[3,256,128]{2,1,0:T(8,128)(2,1)S(1)} %get-tuple-element.7.att, bf16[3,256,128]{2,1,0:T(8,128)(2,1)S(1)} %get-tuple-element.8.att_other, bf16[384,768]{1,0:T(8,128)(2,1)S(1)} %get-tuple-element.9.o_other, ...), custom_call_target="tpu_custom_call" | custom-call | tf_op jit(solution)/shard_map/decoder/pallas_call | solution.py:420

commit v6 on v5

--- a/solution.py
+++ b/solution.py
@@ -85,8 +85,8 @@
 
 def gather(
     emb_h, tally, hidden_h, soft_h, wq_h, wk_h, wv_h, wo_h, gain_h, dq_h, dk_h, dv_h, do_h,
-    latents, att, att_other, o_other,
-    emb, hidden, soft, wq, wk, wv, wo, gain, dq, dk, dv, q_own, k_own, v_own, att_send,
+    wide, att, att_other, o_own, o_other, tokens,
+    latents, emb, hidden, soft, wq, wk, wv, wo, gain, dq, dk, dv, q_own, k_own, v_own, att_send,
     q_scr, k_scr, v_scr, *rest,
 ):
     outs = (rest[0:2], rest[4:6], rest[8:10])
@@ -102,7 +102,7 @@
     for i, (name, source, target) in enumerate((
         ("emb", emb_h, emb), ("wk", wk_h, wk), ("wv", wv_h, wv), ("hidden", hidden_h, hidden), ("wq", wq_h, wq),
         ("soft", soft_h, soft), ("dq", dq_h, dq), ("wo", wo_h, wo), ("gain", gain_h, gain),
-        ("dk", dk_h, dk), ("dv", dv_h, dv),
+        ("dk", dk_h, dk), ("dv", dv_h, dv), ("do", do_h, o_own),
     )):
         loads[name] = pltpu.make_async_copy(source, target, load_sem.at[i])
         loads[name].start()
@@ -213,7 +213,8 @@
         boxes[0][0][pair, own], boxes[0][1][pair, own] = tile(pair, own)
 
     half = slots // 2
-    ready("dq", "wo", "gain", "dk", "dv")
+    ready("dq", "wo", "gain", "dk", "dv", "do")
+    tokens[...] = emb[pl.ds(pl.multiple_of(core * half, half), half), :]
     projected = dot(emb[...], dq[...]).astype(BF16)
     for pair in range(COLOURS):
         q_own[pair] = projected[:, pair * 128 : (pair + 1) * 128]
@@ -318,6 +319,7 @@
     for colour in range(COLOURS):
         forward(colour, latents.at[2 * colour + 1 - core]).wait_recv()
     latent = jnp.concatenate([latents[i].reshape(rows, 128) for i in range(2 * COLOURS)], axis=1)
+    wide[...] = latent.astype(F32)
     for own, weight in ((k_own, dk), (v_own, dv)):
         projected = dot(latent, weight[...]).astype(BF16)
         for pair in range(COLOURS):
@@ -344,29 +346,14 @@
         copy.wait()
 
 
-def decoder(
-    lat, att, att_other, o_other, emb_h, tally, o_own_h,
-    latent_out, tokens, emb, o_own, wide, sem,
-):
-    core = lax.axis_index("qgrp")
-    blocks = lat.shape[0]
+def decoder(wide, att, att_other, o_own, o_other, emb, tally, latent_out, tokens, sem):
     pairs, slots, _ = att.shape
-    loads = [
-        pltpu.make_async_copy(emb_h.at[pl.ds(pl.multiple_of(core * slots, slots), slots)], emb, sem.at[0]),
-        pltpu.make_async_copy(o_own_h, o_own, sem.at[1]),
-    ]
-    for copy in loads:
-        copy.start()
-    for i in range(blocks):
-        wide[:, i * 128 : (i + 1) * 128] = lat[i].astype(F32)
-    write = pltpu.make_async_copy(wide, latent_out, sem.at[2])
+    write = pltpu.make_async_copy(wide, latent_out, sem)
     write.start()
-    for copy in loads:
-        copy.wait()
     own = jnp.concatenate([att[i] for i in range(pairs)], axis=1)
     other = jnp.concatenate([att_other[i] for i in range(pairs)], axis=1)
     update = dot(own, o_own[...]) + dot(other, o_other[...])
-    position = core * slots + lax.broadcasted_iota(jnp.int32, (slots, 1), 0)
+    position = lax.axis_index("qgrp") * slots + lax.broadcasted_iota(jnp.int32, (slots, 1), 0)
     tokens[...] = jnp.where(position < tally[0], emb[...].astype(F32) + update, 0.0)
     write.wait()
 
@@ -388,18 +375,21 @@
             pltpu.VMEM((COLOURS, RING, part, 128), BF16),
             pltpu.VMEM((COLOURS, RING, 8, max(part, 128)), F32),
         ] * 2
-    latents, att, att_other, o_other = pl.pallas_call(
+    passed = pl.pallas_call(
         gather,
         name="gather",
         out_shape=(
-            jax.ShapeDtypeStruct((2 * COLOURS, RING, RING, RING, each, 128), BF16),
+            jax.ShapeDtypeStruct((rows, D), F32),
             jax.ShapeDtypeStruct((COLOURS, half, 128), BF16),
             jax.ShapeDtypeStruct((COLOURS, half, 128), BF16),
             jax.ShapeDtypeStruct(uo.shape, BF16),
+            jax.ShapeDtypeStruct(uo.shape, BF16),
+            jax.ShapeDtypeStruct((half, D), BF16),
         ),
         in_specs=[HBM, SMEM] + [HBM] * 11,
-        out_specs=(VMEM,) * 4,
+        out_specs=(VMEM,) * 6,
         scratch_shapes=[
+            pltpu.VMEM((2 * COLOURS, RING, RING, RING, each, 128), BF16),
             held(emb), held(hidden), pltpu.SMEM(soft.shape, F32), held(gq), held(gk), held(gv), held(go), held(gain),
             held(uq), held(uk), held(uv),
             pltpu.VMEM((COLOURS, slots, 128), BF16),
@@ -412,7 +402,7 @@
             *boxes,
             pltpu.VMEM((each, D), F32),
             pltpu.VMEM((each, D), F32),
-            dma((11,)), dma((3, 2)), dma((3, 2)), dma((3, COLOURS)), dma((2, COLOURS)), dma((COLOURS, RING)),
+            dma((12,)), dma((3, 2)), dma((3, 2)), dma((3, COLOURS)), dma((2, COLOURS)), dma((COLOURS, RING)),
             dma((COLOURS,)), dma((COLOURS,)), dma((5,)), dma((5,)),
         ],
         compiler_params=pltpu.CompilerParams(collective_id=0, has_side_effects=True, vmem_limit_bytes=LIMIT),
@@ -421,11 +411,11 @@
         decoder,
         name="decoder",
         out_shape=(jax.ShapeDtypeStruct((rows, D), F32), jax.ShapeDtypeStruct((half, D), F32)),
-        in_specs=[VMEM] * 4 + [HBM, SMEM, HBM],
+        in_specs=[VMEM] * 6 + [SMEM],
         out_specs=(HBM, VMEM),
-        scratch_shapes=[pltpu.VMEM((half, D), BF16), held(uo), pltpu.VMEM((rows, D), F32), dma((3,))],
-        compiler_params=pltpu.CompilerParams(vmem_limit_bytes=LIMIT),
-    )(latents.reshape(2 * COLOURS, rows, 128), att, att_other, o_other, emb, tally, uo)
+        scratch_shapes=[dma(())],
+        compiler_params=pltpu.CompilerParams(vmem_limit_bytes=16 * 1024 * 1024),
+    )(*passed, tally)
 
 
 def solution(mesh):

time: 51 us -> 51.1 us (level)
  no operation moved by 1% of the time
where the time goes in v6:
time: 51.1 us; the launch traced here: 50.9 us
  Pallas kernels  49.7 us (97%)
  between operations  1.29 us (3%)
    pallas_call x1, Pallas kernels, body(): pl.pallas_call(gather, name='gather', out_shape=(jax.ShapeDtypeStruct((ro...  46.7 us
    pallas_call x1, Pallas kernels, body(): pl.pallas_call(decoder, name='decoder', out_shape=(jax.ShapeDtypeStruct((...  2.94 us

profile of v6, /device:TPU:1, one launch (start us, length us, event | category | flops | bytes accessed | tf_op | source)
XLA Modules:
  0.0 50.9 jit_solution(3241970398561208665)
XLA Ops:
  1.3 46.7 %gather.1 = (f32[1024,768]{1,0:T(8,128)S(1)}, bf16[3,256,128]{2,1,0:T(8,128)(2,1)S(1)}, bf16[3,256,128]{2,1,0:T(8,128)(2,1)S(1)}, bf16[384,768]{1,0:T(8,128)(2,1...) custom-call(bf16[512,768]{1,0:T(8,128)(2,1)} %emb_h.1, s32[1]{0:T(128)S(6)} %copy.15.tally, ...), custom_call_target="tpu_custom_call" | custom-call | tf_op jit(solution)/shard_map/gather/pallas_call | solution.py:378
  48.0 2.9 %decoder.1 = (f32[1024,768]{1,0:T(8,128)}, f32[256,768]{1,0:T(8,128)}) custom-call(f32[1024,768]{1,0:T(8,128)S(1)} %get-tuple-element.8.wide, bf16[3,256,128]{2,1,0:T(8,128)(2,1)S(1)} %get-tuple-element.9.att, bf16[3,256,128]{2,1,0:T(8,128)(2,1)S(1)} %get-tuple-element.10.att_other, bf16[384,768]{1,0:T(8,128)(2,1)S(1)} %get-tuple-element.11.o_own, ...), custom_call_target="tpu_custom_call" | custom-call | tf_op jit(solution)/shard_map/decoder/pallas_call | solution.py:410

commit v7 on v5

--- a/solution.py
+++ b/solution.py
@@ -13,6 +13,7 @@
 HD = 64
 RING = 4
 COLOURS = 3
+PARTS = 4
 REDUCE_AXES = ((0, 1, 2), (1, 2, 0), (2, 0, 1))
 GATHER_AXES = ((2, 1, 0), (0, 2, 1), (1, 0, 2))
 MASKED = -1e30
@@ -357,10 +358,14 @@
     ]
     for copy in loads:
         copy.start()
-    for i in range(blocks):
-        wide[:, i * 128 : (i + 1) * 128] = lat[i].astype(F32)
-    write = pltpu.make_async_copy(wide, latent_out, sem.at[2])
-    write.start()
+    part = wide.shape[0] // PARTS
+    writes = []
+    for r in range(PARTS):
+        for i in range(blocks):
+            wide[r * part : (r + 1) * part, i * 128 : (i + 1) * 128] = lat[i, r * part : (r + 1) * part].astype(F32)
+        at = pl.ds(r * part, part)
+        writes.append(pltpu.make_async_copy(wide.at[at], latent_out.at[at], sem.at[2 + r]))
+        writes[-1].start()
     for copy in loads:
         copy.wait()
     own = jnp.concatenate([att[i] for i in range(pairs)], axis=1)
@@ -368,7 +373,8 @@
     update = dot(own, o_own[...]) + dot(other, o_other[...])
     position = core * slots + lax.broadcasted_iota(jnp.int32, (slots, 1), 0)
     tokens[...] = jnp.where(position < tally[0], emb[...].astype(F32) + update, 0.0)
-    write.wait()
+    for copy in writes:
+        copy.wait()
 
 
 def body(emb, tally, hidden, soft, gq, gk, gv, go, uq, uk, uv, uo, gain):
@@ -423,7 +429,7 @@
         out_shape=(jax.ShapeDtypeStruct((rows, D), F32), jax.ShapeDtypeStruct((half, D), F32)),
         in_specs=[VMEM] * 4 + [HBM, SMEM, HBM],
         out_specs=(HBM, VMEM),
-        scratch_shapes=[pltpu.VMEM((half, D), BF16), held(uo), pltpu.VMEM((rows, D), F32), dma((3,))],
+        scratch_shapes=[pltpu.VMEM((half, D), BF16), held(uo), pltpu.VMEM((rows, D), F32), dma((2 + PARTS,))],
         compiler_params=pltpu.CompilerParams(vmem_limit_bytes=LIMIT),
     )(latents.reshape(2 * COLOURS, rows, 128), att, att_other, o_other, emb, tally, uo)
 

time: 51 us -> 51.4 us (level)
  no operation moved by 1% of the time
where the time goes in v7:
time: 51.4 us; the launch traced here: 51.3 us
  Pallas kernels  50 us (97%)
  between operations  1.29 us (3%)
    pallas_call x1, Pallas kernels, body(): pl.pallas_call(gather, name='gather', out_shape=(jax.ShapeDtypeStruct((2...  46.7 us
    pallas_call x1, Pallas kernels, body(): pl.pallas_call(decoder, name='decoder', out_shape=(jax.ShapeDtypeStruct((...  3.29 us

profile of v7, /device:TPU:1, one launch (start us, length us, event | category | flops | bytes accessed | tf_op | source)
XLA Modules:
  0.0 51.3 jit_solution(560758656033007835)
XLA Ops:
  1.3 46.7 %gather.1 = (bf16[6,4,4,4,16,128]{5,4,3,2,1,0:T(8,128)(2,1)S(1)}, bf16[3,256,128]{2,1,0:T(8,128)(2,1)S(1)}, bf16[3,256,128]{2,1,0:T(8,128)(2,1)S(1)}, bf16[384,768]{1,0:T(8,128)(2,1)S(1)}) custom-call(bf16[512,768]{1,0:T(8,128)(2,1)} %emb_h.3, s32[1]{0:T(128)S(6)} %copy.15.tally, bf16[1024,768]{1,0:T(8,128)(2,1)} %hidden_h.1, f32[2,12]{1,0:T(2,128)} %soft_h.1, ...), custom_call_target="tpu_custom_call" | custom-call | tf_op jit(solution)/shard_map/gather/pallas_call | solution.py:397
  48.0 3.3 %decoder.1 = (f32[1024,768]{1,0:T(8,128)}, f32[256,768]{1,0:T(8,128)}) custom-call(bf16[6,1024,128]{2,1,0:T(8,128)(2,1)S(1)} %bitcast.1, bf16[3,256,128]{2,1,0:T(8,128)(2,1)S(1)} %get-tuple-element.7.att, bf16[3,256,128]{2,1,0:T(8,128)(2,1)S(1)} %get-tuple-element.8.att_other, bf16[384,768]{1,0:T(8,128)(2,1)S(1)} %get-tuple-element.9.o_other, ...), custom_call_target="tpu_custom_call" | custom-call | tf_op jit(solution)/shard_map/decoder/pallas_call | solution.py:426
